TPU v7x, 512 devices: a whole 4x4x16 slice. The times are simulated.
512 devices in a mesh: rows: 128 (over z, x, core), half: 4 (over y).
Axes of the slice: x: 4, y: 4, z: 16, core: 2. Of those that a mesh axis runs over, the one named last changes fastest.
Arguments:
- micrograph: bfloat16 [4096, 4096], P('rows', 'half'), may hold values from -6 to 6
- box_tops: int32 [128, 4, 4, 2], replicated, may hold values from 0 to 3840, as said below
- box_live: int32 [128, 4, 4], replicated, may hold values from 0 to 1, as said below
- box_class: int32 [128, 4, 4], replicated, may hold values from 0 to 49
- box_shift: int32 [128, 4, 4, 2], P('rows', 'half'), may hold values from -8 to 8
Outputs:
- power: float32 [4, 1024, 4096], P('half', 'rows')
- class_means: float32 [50, 2, 256, 256], P(None, None, 'rows', 'half')
Inputs may be any that keep to these rules, and one draw needn't show every extreme that they name: `box_tops`: the box of every slot lies inside the micrograph. A slot of box_live = 1 at index (i, j, s) has its first row among rows i * 32 to (i + 1) * 32 - 1. `box_live`: in each device's slots the live ones come first; in every draw some device has all 4 slots live.
All inputs are finite; a program needn't handle non-finite values.
Results may differ from a plain program's by a relative error of at most 0.0029.
Values may be sent and summed in bfloat16 or wider, within the bound.
A program may use at most 64 MiB of HBM per device.

v0:
```python
import jax
import jax.numpy as jnp
from jax import lax
from jax.sharding import PartitionSpec as P

BOX = 256
CLASSES = 50
RADIX = 64


highest = lax.Precision.HIGHEST


def in_order(pieces, dim):
    pieces = jnp.moveaxis(pieces, 0, dim)
    shape = pieces.shape
    return pieces.reshape(*shape[:dim], shape[dim] * shape[dim + 1], *shape[dim + 2 :])


def from_everyone(array, axis):
    count = lax.axis_size(axis)
    return lax.all_to_all(
        jnp.broadcast_to(array[None], (count, *array.shape)), axis, 0, 0, tiled=True
    )


def gathered_copies(array, axis, dim):
    return in_order(from_everyone(array, axis), dim)


def passed_along(block, axis, distance):
    devices = range(lax.axis_size(axis))
    route = [(i - distance, i) for i in devices if i - distance in devices]
    return lax.ppermute(block, axis, route)


def split_up(array, dim, count):
    before, after = (array.shape[:dim], array.shape[dim + 1 :])
    return jnp.moveaxis(array.reshape(*before, count, -1, *after), dim, 0)


def sum_at_owner(array, axis, dim):
    count = lax.axis_size(axis)
    pieces = lax.all_to_all(split_up(array, dim, count), axis, 0, 0, tiled=True)
    return jnp.sum(pieces, axis=0)


def phases(left_index, right_index, length):
    rotations = jnp.mod(left_index[:, None] * right_index[None, :], length)
    angles = 2.0 * jnp.pi / length * rotations.astype(jnp.float32)
    return (jnp.cos(angles), jnp.sin(angles))


def product(pattern, left_side, matrix):
    return jnp.einsum(pattern, left_side, matrix, precision=highest)


def four_step(real_part, imag_part, first_index, how_many, rows_last):
    height = real_part.shape[0]
    length = real_part.shape[1]
    outer_size = RADIX
    inner_size = length // outer_size
    real_part = real_part.reshape(height, outer_size, inner_size)
    spread = jnp.arange(outer_size, dtype=jnp.int32)
    across = jnp.arange(inner_size, dtype=jnp.int32)
    cos_one, sin_one = phases(spread, spread, outer_size)
    section_real = product("mab,ka->mkb", real_part, cos_one)
    section_imag = -product("mab,ka->mkb", real_part, sin_one)
    if imag_part is not None:
        imag_part = imag_part.reshape(height, outer_size, inner_size)
        section_real = section_real + product("mab,ka->mkb", imag_part, sin_one)
        section_imag = section_imag + product("mab,ka->mkb", imag_part, cos_one)
    twist_cos, twist_sin = phases(spread, across, length)
    turned_real = section_real * twist_cos + section_imag * twist_sin
    turned_imag = section_imag * twist_cos - section_real * twist_sin
    wanted = first_index + jnp.arange(how_many, dtype=jnp.int32)
    cos_two, sin_two = phases(wanted, across, inner_size)
    pattern = "mkb,tb->tkm" if rows_last else "mkb,tb->mtk"
    out_real = product(pattern, turned_real, cos_two) + product(pattern, turned_imag, sin_two)
    out_imag = product(pattern, turned_imag, cos_two) - product(pattern, turned_real, sin_two)
    return (out_real, out_imag)


def per_device(micrograph, box_tops, box_live, box_class, box_shift):
    row_index = lax.axis_index("rows")
    half_index = lax.axis_index("half")
    band_rows = gathered_copies(micrograph, "half", 1)
    height = band_rows.shape[0]
    full_width = band_rows.shape[1]
    quarter = full_width // lax.axis_size("half")
    per_block = quarter // RADIX
    image_rows = band_rows.astype(jnp.float32)
    part_real, part_imag = four_step(image_rows, None, half_index * per_block, per_block, True)
    partial_value = jnp.stack(
        [part_real.reshape(quarter, height), part_imag.reshape(quarter, height)]
    )
    columns = lax.all_to_all(partial_value, "rows", split_axis=1, concat_axis=2, tiled=True)
    column_count = columns.shape[1]
    freq_real, freq_imag = four_step(columns[0], columns[1], 0, full_width // RADIX, False)
    power_out = (freq_real * freq_real + freq_imag * freq_imag).reshape(1, column_count, full_width)
    power_out = power_out / (full_width * full_width)
    local_tops = box_tops[row_index, half_index]
    start_rows = local_tops[:, 0] - row_index * height
    start_cols = local_tops[:, 1]
    reach_bands = (BOX + height - 2) // height
    pieces = [band_rows]
    for offset in range(1, reach_bands + 1):
        pieces.append(passed_along(band_rows, "rows", -offset))
    stacked = jnp.concatenate(pieces, axis=0)
    particle_boxes = jax.vmap(
        lambda corner_row, corner_col: lax.dynamic_slice(
            stacked, (corner_row, corner_col), (BOX, BOX)
        )
    )(start_rows, start_cols)
    frequency = jnp.arange(BOX, dtype=jnp.int32)
    cos_box, sin_box = phases(frequency, frequency, BOX)
    local_offsets = box_shift.reshape(-1, 2)

    def spectrum(member):
        particle, offsets_pair = member
        values = particle.astype(jnp.float32)
        inner_real = jnp.dot(values, cos_box, precision=highest)
        inner_imag = -jnp.dot(values, sin_box, precision=highest)
        outer_real = (
            jnp.dot(cos_box, inner_real, precision=highest)
            + jnp.dot(sin_box, inner_imag, precision=highest)
        ) / BOX
        outer_imag = (
            jnp.dot(cos_box, inner_imag, precision=highest)
            - jnp.dot(sin_box, inner_real, precision=highest)
        ) / BOX
        rotations = jnp.mod(
            frequency[:, None] * offsets_pair[0] + frequency[None, :] * offsets_pair[1], BOX
        )
        angles = 2.0 * jnp.pi / BOX * rotations.astype(jnp.float32)
        ramp_cos = jnp.cos(angles)
        ramp_sin = jnp.sin(angles)
        shifted_real = outer_real * ramp_cos + outer_imag * ramp_sin
        shifted_imag = outer_imag * ramp_cos - outer_real * ramp_sin
        return jnp.stack([shifted_real, shifted_imag]).astype(jnp.bfloat16)

    spectra = lax.map(spectrum, (particle_boxes, local_offsets))
    classes_all = jnp.arange(CLASSES, dtype=jnp.int32)
    all_labels = box_class.reshape(-1)
    all_live = box_live.reshape(-1)
    counts = jnp.sum(
        (all_labels[None, :] == classes_all[:, None]).astype(jnp.int32) * all_live[None, :], axis=1
    )
    arrived = lax.all_to_all(spectra, "rows", split_axis=2, concat_axis=0, tiled=True)
    chosen_labels = box_class[:, half_index].reshape(-1)
    chosen_live = box_live[:, half_index].reshape(-1)
    weights = (
        (chosen_labels[None, :] == classes_all[:, None]).astype(jnp.int32) * chosen_live[None, :]
    ).astype(jnp.bfloat16)
    flat_spectra = arrived.reshape(arrived.shape[0], -1)
    partial_sums = jnp.dot(weights, flat_spectra, preferred_element_type=jnp.float32)
    partial_sums = partial_sums.reshape((CLASSES,) + arrived.shape[1:])
    class_sums = sum_at_owner(partial_sums, "half", 3)
    divisor = jnp.maximum(counts, 1).astype(jnp.float32)
    class_means = class_sums / divisor[:, None, None, None]
    return (power_out, class_means)


def solution(mesh):
    in_specs = (P("rows", "half"), P(), P(), P(), P("rows", "half", None, None))
    out_specs = (P("half", "rows", None), P(None, None, "rows", "half"))
    return jax.shard_map(
        per_device, mesh=mesh, in_specs=in_specs, out_specs=out_specs, check_vma=False
    )
```

profile of v0, /device:TPU:1, one launch (start us, length us, event | category | flops | bytes accessed | tf_op | source)
XLA Modules:
  0.0 246.8 jit_solution(14791376599436781870)
XLA Ops:
  2.2 5.0 %all-to-all-start = ((bf16[4,32,1024]{2,1,0:T(8,128)(2,1)}), bf16[4,32,1024]{2,1,0:T(8,128)(2,1)S(1)}, u32[]{:S(2)}, u32[]{:S(2)}) async-start(bf16[4,32,1024]{2,1,0:T(8,128)(2,1)} %broadcast_in_dim.5), calls=%async_computation | async-start | bytes 524288 | tf_op jit(solution)/shard_map/all_to_all | solution.py:22
  7.6 5.2 %all-to-all-done = bf16[4,32,1024]{2,1,0:T(8,128)(2,1)S(1)} async-done(((bf16[4,32,1024]{2,1,0:T(8,128)(2,1)}), bf16[4,32,1024]{2,1,0:T(8,128)(2,1)S(1)}, u32[]{:S(2)}, u32[]{:S(2)}) %all-to-all-start) | async-done | bytes 262176 | tf_op jit(solution)/shard_map/all_to_all | solution.py:22
  12.8 8.3 %collective-permute-start = (bf16[32,4096]{1,0:T(8,128)(2,1)S(1)}, bf16[32,4096]{1,0:T(8,128)(2,1)}, u32[]{:S(2)}, u32[]{:S(2)}) collective-permute-start(bf16[32,4096]{1,0:T(8,128)(2,1)S(1)} %bitcast.162), channel_id=1, source_target_pairs={{4,0},{8,4},{12,8},{16,12},{20,16},{24,20},{28,24},{32,28},{36,32}... | collective-permute-start | bytes 786440 | tf_op jit(solution)/shard_map/ppermute | solution.py:34
  28.2 2.6 %fusion.73 = f32[16,32,64]{2,0,1:T(8,128)S(1)} fusion(f32[64,32,64]{2,0,1:T(8,128)S(1)} %convolution_negate_fusion.1, f32[64,32,64]{2,0,1:T(8,128)S(1)} %fusion.100, f32[64,64]{1,0:T(8,128)S(1)} %get-tuple-element.188, f32[64,64]{1,0:T(8,128)S(1)} %get-tuple-element.189, s32[16]{0:T(128)S(1)} %iota_add_fusion), kind=kOutput, calls=%fused_computation.93 | convolution fusion | flops 25573376 | bytes 1212480 | tf_op jit(solution)/shard_map/mkb,tb->tkm/dot_general | solution.py:55
  30.8 2.6 %fusion.69 = f32[16,32,64]{2,0,1:T(8,128)S(1)} fusion(f32[64,32,64]{2,0,1:T(8,128)S(1)} %fusion.100, f32[64,32,64]{2,0,1:T(8,128)S(1)} %convolution_negate_fusion.1, f32[64,64]{1,0:T(8,128)S(1)} %get-tuple-element.188, f32[64,64]{1,0:T(8,128)S(1)} %get-tuple-element.189, s32[16]{0:T(128)S(1)} %iota_add_fusion), kind=kOutput, calls=%fused_computation.89 | convolution fusion | flops 25573376 | bytes 1212480 | tf_op jit(solution)/shard_map/mkb,tb->tkm/dot_general | solution.py:55
  33.4 2.6 %fusion.68 = f32[16,64,32]{1,0,2:T(8,128)S(1)} fusion(f32[16,32,64]{2,0,1:T(8,128)S(1)} %fusion.73, f32[64,32,64]{2,0,1:T(8,128)S(1)} %fusion.100, f32[64,32,64]{2,0,1:T(8,128)S(1)} %convolution_negate_fusion.1, f32[64,64]{1,0:T(8,128)S(1)} %get-tuple-element.188, f32[64,64]{1,0:T(8,128)S(1)} %get-tuple-element.189, s32[16]{0:T(128)S(1)} %iota_add_fusion), kind=kOutput, calls=%fused_computation.88 | convolution fusion | flops 25606144 | bytes 1343552 | tf_op jit(solution)/shard_map/mkb,tb->tkm/dot_general | solution.py:55
  36.2 2.6 %fusion.67 = f32[16,64,32]{1,0,2:T(8,128)S(1)} fusion(f32[16,32,64]{2,0,1:T(8,128)S(1)} %fusion.69, f32[64,32,64]{2,0,1:T(8,128)S(1)} %convolution_negate_fusion.1, f32[64,32,64]{2,0,1:T(8,128)S(1)} %fusion.100, f32[64,64]{1,0:T(8,128)S(1)} %get-tuple-element.188, f32[64,64]{1,0:T(8,128)S(1)} %get-tuple-element.189, s32[16]{0:T(128)S(1)} %iota_add_fusion), kind=kOutput, calls=%fused_computation.86 | convolution fusion | flops 25606144 | bytes 1343552 | tf_op jit(solution)/shard_map/mkb,tb->tkm/dot_general | solution.py:55
  41.3 23.4 %all-to-all-start.1 = ((f32[128,1,512]{2,1,0:T(1,128)}), f32[128,1,512]{2,1,0:T(1,128)S(1)}, u32[]{:S(2)}, u32[]{:S(2)}) async-start(f32[128,1,512]{2,1,0:T(1,128)} %reshape.168), calls=%async_computation.1 | async-start | bytes 524288 | tf_op jit(solution)/shard_map/all_to_all | solution.py:97
  72.8 3.1 %collective-permute-done.5 = bf16[32,4096]{1,0:T(8,128)(2,1)S(1)} collective-permute-done((bf16[32,4096]{1,0:T(8,128)(2,1)S(1)}, bf16[32,4096]{1,0:T(8,128)(2,1)S(1)}, u32[]{:S(2)}, u32[]{:S(2)}) %collective-permute-start.5) | collective-permute-done | bytes 262176 | tf_op jit(solution)/shard_map/ppermute | solution.py:34
  76.0 13.5 %collective-permute-done.6 = bf16[32,4096]{1,0:T(8,128)(2,1)S(1)} collective-permute-done((bf16[32,4096]{1,0:T(8,128)(2,1)S(1)}, bf16[32,4096]{1,0:T(8,128)(2,1)S(1)}, u32[]{:S(2)}, u32[]{:S(2)}) %collective-permute-start.6) | collective-permute-done | bytes 262176 | tf_op jit(solution)/shard_map/ppermute | solution.py:34
  89.4 4.7 %collective-permute-done.7 = bf16[32,4096]{1,0:T(8,128)(2,1)S(1)} collective-permute-done((bf16[32,4096]{1,0:T(8,128)(2,1)S(1)}, bf16[32,4096]{1,0:T(8,128)(2,1)S(1)}, u32[]{:S(2)}, u32[]{:S(2)}) %collective-permute-start.7) | collective-permute-done | bytes 262176 | tf_op jit(solution)/shard_map/ppermute | solution.py:34
  94.2 10.4 %while.15 = (s32[]{:T(128)}, bf16[288,4096]{1,0:T(8,128)(2,1)S(1)}, s32[4,2]{0,1:T(2,128)S(1)}, bf16[4,256,256]{2,1,0:T(8,128)(2,1)}, s32[]{:T(128)}) while((s32[]{:T(128)}, bf16[288,4096]{1,0:T(8,128)(2,1)S(1)}, s32[4,2]{0,1:T(2,128)S(1)}, bf16[4,256,256]{2,1,0:T(8,128)(2,1)}, s32[]{:T(128)}) %tuple.66), condition=%wide.while_cond, body=%wide.while_body.sunk | while | flops 2 | bytes 263777 | solution.py:111
  104.6 57.0 %while.16 = (s32[]{:T(128)}, bf16[4,2,256,256]{3,1,0,2:T(2,128)(2,1)}, bf16[4,256,256]{2,1,0:T(8,128)(2,1)}, s32[4,2]{0,1:T(2,128)S(1)}, s32[]{:T(128)}) while((s32[]{:T(128)}, bf16[4,2,256,256]{3,1,0,2:T(2,128)(2,1)}, bf16[4,256,256]{2,1,0:T(8,128)(2,1)}, s32[4,2]{0,1:T(2,128)S(1)}, s32[]{:T(128)}) %tuple.72), condition=%wide.region_1.2_spmd.clone.clone, body=%wide.region_0.1_spmd.clone.clone.sunk | while | flops 1215365632 | bytes 5248617 | solution.py:142
  104.6 2.2 convolution_negate_fusion.4
  115.2 2.5 %fusion.249 = (bf16[1,1,256,256]{2,3,1,0:T(8,128)(2,1)S(1)}, bf16[1,1,256,256]{2,3,1,0:T(8,128)(2,1)S(1)}) fusion(f32[256,256]{0,1:T(8,128)S(1)} %fusion.246, s32[256]{0:T(256)S(1)} %get-tuple-element.254, s32[256]{0:T(256)S(1)} %get-tuple-element.255, f32[256,256]{1,0:T(8,128)S(1)} %fusion.248, f32[256,256]{1,0:T(8,128)S(1)} %convolution_negate_fusion.4), kind=kOutput, calls=%fused_computation.32.clone.1 | convolution fusion | flops 203816960 | bytes 1050624 | tf_op jit(solution)/shard_map/while/body/eval_jaxpr/dot_general | solution.py:126
  129.4 2.5 %fusion.249 = (bf16[1,1,256,256]{2,3,1,0:T(8,128)(2,1)S(1)}, bf16[1,1,256,256]{2,3,1,0:T(8,128)(2,1)S(1)}) fusion(f32[256,256]{0,1:T(8,128)S(1)} %fusion.246, s32[256]{0:T(256)S(1)} %get-tuple-element.254, s32[256]{0:T(256)S(1)} %get-tuple-element.255, f32[256,256]{1,0:T(8,128)S(1)} %fusion.248, f32[256,256]{1,0:T(8,128)S(1)} %convolution_negate_fusion.4), kind=kOutput, calls=%fused_computation.32.clone.1 | convolution fusion | flops 203816960 | bytes 1050624 | tf_op jit(solution)/shard_map/while/body/eval_jaxpr/dot_general | solution.py:126
  133.1 2.2 convolution_negate_fusion.4
  143.7 2.5 %fusion.249 = (bf16[1,1,256,256]{2,3,1,0:T(8,128)(2,1)S(1)}, bf16[1,1,256,256]{2,3,1,0:T(8,128)(2,1)S(1)}) fusion(f32[256,256]{0,1:T(8,128)S(1)} %fusion.246, s32[256]{0:T(256)S(1)} %get-tuple-element.254, s32[256]{0:T(256)S(1)} %get-tuple-element.255, f32[256,256]{1,0:T(8,128)S(1)} %fusion.248, f32[256,256]{1,0:T(8,128)S(1)} %convolution_negate_fusion.4), kind=kOutput, calls=%fused_computation.32.clone.1 | convolution fusion | flops 203816960 | bytes 1050624 | tf_op jit(solution)/shard_map/while/body/eval_jaxpr/dot_general | solution.py:126
  147.4 2.2 convolution_negate_fusion.4
  158.0 2.5 %fusion.249 = (bf16[1,1,256,256]{2,3,1,0:T(8,128)(2,1)S(1)}, bf16[1,1,256,256]{2,3,1,0:T(8,128)(2,1)S(1)}) fusion(f32[256,256]{0,1:T(8,128)S(1)} %fusion.246, s32[256]{0:T(256)S(1)} %get-tuple-element.254, s32[256]{0:T(256)S(1)} %get-tuple-element.255, f32[256,256]{1,0:T(8,128)S(1)} %fusion.248, f32[256,256]{1,0:T(8,128)S(1)} %convolution_negate_fusion.4), kind=kOutput, calls=%fused_computation.32.clone.1 | convolution fusion | flops 203816960 | bytes 1050624 | tf_op jit(solution)/shard_map/while/body/eval_jaxpr/dot_general | solution.py:126
  161.6 15.8 %all-to-all-start.2 = ((bf16[4,2,256,256]{3,1,0,2:T(2,128)(2,1)}), bf16[4,2,256,256]{3,1,0,2:T(2,128)(2,1)S(1)}, u32[]{:S(2)}, u32[]{:S(2)}) async-start(bf16[4,2,256,256]{3,1,0,2:T(2,128)(2,1)} %get-tuple-element.107), calls=%async_computation.2 | async-start | bytes 2097152 | tf_op jit(solution)/shard_map/all_to_all | solution.py:149
  187.2 42.2 %all-to-all-done.2 = bf16[4,2,256,256]{3,1,0,2:T(2,128)(2,1)S(1)} async-done(((bf16[4,2,256,256]{3,1,0,2:T(2,128)(2,1)}), bf16[4,2,256,256]{3,1,0,2:T(2,128)(2,1)S(1)}, u32[]{:S(2)}, u32[]{:S(2)}) %all-to-all-start.2) | async-done | bytes 1048608 | tf_op jit(solution)/shard_map/all_to_all | solution.py:149
  235.7 3.4 %all-to-all-start.3 = ((f32[4,1,12800]{2,1,0:T(1,128)}), f32[4,1,12800]{2,1,0:T(1,128)S(1)}, u32[]{:S(2)}, u32[]{:S(2)}) async-start(f32[4,1,12800]{2,1,0:T(1,128)} %reshape.170), calls=%async_computation.3 | async-start | bytes 409600 | tf_op jit(solution)/shard_map/all_to_all | solution.py:44
  240.8 3.4 %all-to-all-done.3 = f32[4,1,12800]{2,1,0:T(1,128)S(1)} async-done(((f32[4,1,12800]{2,1,0:T(1,128)}), f32[4,1,12800]{2,1,0:T(1,128)S(1)}, u32[]{:S(2)}, u32[]{:S(2)}) %all-to-all-start.3) | async-done | bytes 204832 | tf_op jit(solution)/shard_map/all_to_all | solution.py:44
  (142 shorter events, 90.4 us)
Async XLA Ops:
  0.6 6.6 %copy-start = (s32[128,4,4,2]{0,3,2,1:T(2,128)S(1)}, s32[128,4,4,2]{0,3,2,1:T(2,128)}, u32[]{:S(2)}) copy-start(s32[128,4,4,2]{0,3,2,1:T(2,128)} %param.8) | copy-start | bytes 49156
  2.2 10.5 %all-to-all-start = ((bf16[4,32,1024]{2,1,0:T(8,128)(2,1)}), bf16[4,32,1024]{2,1,0:T(8,128)(2,1)S(1)}, u32[]{:S(2)}, u32[]{:S(2)}) async-start(bf16[4,32,1024]{2,1,0:T(8,128)(2,1)} %broadcast_in_dim.5), calls=%async_computation | async-start | bytes 524288 | tf_op jit(solution)/shard_map/all_to_all | solution.py:22
  12.8 52.0 %collective-permute-start = (bf16[32,4096]{1,0:T(8,128)(2,1)S(1)}, bf16[32,4096]{1,0:T(8,128)(2,1)}, u32[]{:S(2)}, u32[]{:S(2)}) collective-permute-start(bf16[32,4096]{1,0:T(8,128)(2,1)S(1)} %bitcast.162), channel_id=1, source_target_pairs={{4,0},{8,4},{12,8},{16,12},{20,16},{24,20},{28,24},{32,28},{36,32}... | collective-permute-start | bytes 786440 | tf_op jit(solution)/shard_map/ppermute | solution.py:34
  21.0 46.0 %collective-permute-start.1 = (bf16[32,4096]{1,0:T(8,128)(2,1)S(1)}, bf16[32,4096]{1,0:T(8,128)(2,1)}, u32[]{:S(2)}, u32[]{:S(2)}) collective-permute-start(bf16[32,4096]{1,0:T(8,128)(2,1)S(1)} %bitcast.163), channel_id=1, source_target_pairs={{8,0},{12,4},{16,8},{20,12},{24,16},{28,20},{32,24},{36,28},{40,32... | collective-permute-start | bytes 786440 | tf_op jit(solution)/shard_map/ppermute | solution.py:34
  22.3 47.0 %collective-permute-start.2 = (bf16[32,4096]{1,0:T(8,128)(2,1)S(1)}, bf16[32,4096]{1,0:T(8,128)(2,1)}, u32[]{:S(2)}, u32[]{:S(2)}) collective-permute-start(bf16[32,4096]{1,0:T(8,128)(2,1)S(1)} %bitcast.164), channel_id=1, source_target_pairs={{12,0},{16,4},{20,8},{24,12},{28,16},{32,20},{36,24},{40,28},{44,3... | collective-permute-start | bytes 786440 | tf_op jit(solution)/shard_map/ppermute | solution.py:34
  23.6 48.1 %collective-permute-start.3 = (bf16[32,4096]{1,0:T(8,128)(2,1)S(1)}, bf16[32,4096]{1,0:T(8,128)(2,1)}, u32[]{:S(2)}, u32[]{:S(2)}) collective-permute-start(bf16[32,4096]{1,0:T(8,128)(2,1)S(1)} %bitcast.165), channel_id=1, source_target_pairs={{16,0},{20,4},{24,8},{28,12},{32,16},{36,20},{40,24},{44,28},{48,3... | collective-permute-start | bytes 786440 | tf_op jit(solution)/shard_map/ppermute | solution.py:34
  24.9 47.8 %collective-permute-start.4 = (bf16[32,4096]{1,0:T(8,128)(2,1)S(1)}, bf16[32,4096]{1,0:T(8,128)(2,1)S(1)}, u32[]{:S(2)}, u32[]{:S(2)}) collective-permute-start(bf16[32,4096]{1,0:T(8,128)(2,1)S(1)} %bitcast.166), channel_id=1, source_target_pairs={{20,0},{24,4},{28,8},{32,12},{36,16},{40,20},{44,24},{48,28},{52,3... | collective-permute-start | bytes 786440 | tf_op jit(solution)/shard_map/ppermute | solution.py:34
  41.3 120.3 %all-to-all-start.1 = ((f32[128,1,512]{2,1,0:T(1,128)}), f32[128,1,512]{2,1,0:T(1,128)S(1)}, u32[]{:S(2)}, u32[]{:S(2)}) async-start(f32[128,1,512]{2,1,0:T(1,128)} %reshape.168), calls=%async_computation.1 | async-start | bytes 524288 | tf_op jit(solution)/shard_map/all_to_all | solution.py:97
  64.7 11.2 %collective-permute-start.5 = (bf16[32,4096]{1,0:T(8,128)(2,1)S(1)}, bf16[32,4096]{1,0:T(8,128)(2,1)S(1)}, u32[]{:S(2)}, u32[]{:S(2)}) collective-permute-start(bf16[32,4096]{1,0:T(8,128)(2,1)S(1)} %bitcast.168), channel_id=1, source_target_pairs={{24,0},{28,4},{32,8},{36,12},{40,16},{44,20},{48,24},{52,28},{56,3... | collective-permute-start | bytes 786440 | tf_op jit(solution)/shard_map/ppermute | solution.py:34
  67.0 22.4 %collective-permute-start.6 = (bf16[32,4096]{1,0:T(8,128)(2,1)S(1)}, bf16[32,4096]{1,0:T(8,128)(2,1)S(1)}, u32[]{:S(2)}, u32[]{:S(2)}) collective-permute-start(bf16[32,4096]{1,0:T(8,128)(2,1)S(1)} %bitcast.169), channel_id=1, source_target_pairs={{28,0},{32,4},{36,8},{40,12},{44,16},{48,20},{52,24},{56,28},{60,3... | collective-permute-start | bytes 786440 | tf_op jit(solution)/shard_map/ppermute | solution.py:34
  69.3 35.3 %copy-start.1 = (s32[1,1,4,2]{2,3,1,0:T(2,128)S(1)}, s32[1,1,4,2]{2,3,1,0:T(2,128)}, u32[]{:S(2)}) copy-start(s32[1,1,4,2]{2,3,1,0:T(2,128)} %param.11) | copy-start | bytes 100
  69.3 24.9 %collective-permute-start.7 = (bf16[32,4096]{1,0:T(8,128)(2,1)S(1)}, bf16[32,4096]{1,0:T(8,128)(2,1)S(1)}, u32[]{:S(2)}, u32[]{:S(2)}) collective-permute-start(bf16[32,4096]{1,0:T(8,128)(2,1)S(1)} %bitcast.170), channel_id=1, source_target_pairs={{32,0},{36,4},{40,8},{44,12},{48,16},{52,20},{56,24},{60,28},{64,3... | collective-permute-start | bytes 786440 | tf_op jit(solution)/shard_map/ppermute | solution.py:34
  104.6 72.8 %copy-start.3 = (s32[128,4,4]{0,2,1:T(4,128)S(1)}, s32[128,4,4]{0,2,1:T(4,128)}, u32[]{:S(2)}) copy-start(s32[128,4,4]{0,2,1:T(4,128)} %param.10) | copy-start | bytes 24580
  161.6 16.0 %copy-start.2 = (s32[128,4,4]{0,2,1:T(4,128)S(1)}, s32[128,4,4]{0,2,1:T(4,128)}, u32[]{:S(2)}) copy-start(s32[128,4,4]{0,2,1:T(4,128)} %param.9) | copy-start | bytes 24580
  161.6 67.9 %all-to-all-start.2 = ((bf16[4,2,256,256]{3,1,0,2:T(2,128)(2,1)}), bf16[4,2,256,256]{3,1,0,2:T(2,128)(2,1)S(1)}, u32[]{:S(2)}, u32[]{:S(2)}) async-start(bf16[4,2,256,256]{3,1,0,2:T(2,128)(2,1)} %get-tuple-element.107), calls=%async_computation.2 | async-start | bytes 2097152 | tf_op jit(solution)/shard_map/all_to_all | solution.py:149
  235.7 8.6 %all-to-all-start.3 = ((f32[4,1,12800]{2,1,0:T(1,128)}), f32[4,1,12800]{2,1,0:T(1,128)S(1)}, u32[]{:S(2)}, u32[]{:S(2)}) async-start(f32[4,1,12800]{2,1,0:T(1,128)} %reshape.170), calls=%async_computation.3 | async-start | bytes 409600 | tf_op jit(solution)/shard_map/all_to_all | solution.py:44
where the time goes:
time: 251 us; the launch traced here: 247 us
  waiting for transfers between devices  72.2 us (29%)
  starting transfers between devices  65.1 us (26%)
  matrix products  63.4 us (25%)
  local copies, waits for them, and re-layouts  36.7 us (15%)
  other arithmetic  8.04 us (3%)
    all_to_all x1, waiting for transfers between devices, per_device(): lax.all_to_all(spectra, 'rows', split_axis=2, concat_axis=0, tiled=True)  42.2 us
    all_to_all x1, starting transfers between devices, per_device(): lax.all_to_all(partial_value, 'rows', split_axis=1, concat_axis=2, tiled=...  23.4 us
    ppermute x8, waiting for transfers between devices, passed_along(): return lax.ppermute(block, axis, route)  21.4 us
    dot_general x14, matrix products, product(): return jnp.einsum(pattern, left_side, matrix, precision=highest)  17.8 us
    ppermute x8, starting transfers between devices, passed_along(): return lax.ppermute(block, axis, route)  17.5 us
    all_to_all x1, starting transfers between devices, per_device(): lax.all_to_all(spectra, 'rows', split_axis=2, concat_axis=0, tiled=True)  15.8 us
    gather x12, local copies, waits for them, and re-layouts  10.4 us
    dot_general x4, matrix products, spectrum(): jnp.dot(sin_box, inner_imag, precision=highest)  9.95 us
  transfers between devices with their start and end apart: 12, of which 6 were waited for; matrix products, arithmetic and copies ran while one was open for 40% of the time, Pallas kernels for 0%

commit v1 on v0

v1 whole, which is shorter than its diff:
```python
import functools

import jax
import jax.numpy as jnp
import numpy as np
from jax import lax
from jax.experimental import pallas as pl
from jax.experimental.pallas import tpu as pltpu
from jax.sharding import PartitionSpec as P

BOX = 256
CLASSES = 50
NPIX = 4096
NZ, NQ, NY = 16, 8, 4
NBAND = 128
REACH = 9
MESH = pl.DeviceIdType.MESH
f32 = jnp.float32
bf16 = jnp.bfloat16
VMEM = pl.BlockSpec(memory_space=pltpu.VMEM)
SMEM = pl.BlockSpec(memory_space=pltpu.SMEM)
ANY = pl.BlockSpec(memory_space=pl.ANY)


def two_parts(matrix):
    high = matrix.astype(bf16)
    return np.stack([high, (matrix - high.astype(np.float64)).astype(bf16)])


def turn(left, right, length):
    angle = 2.0 * np.pi / length * np.mod(np.multiply.outer(left, right), length)
    return np.cos(angle), np.sin(angle)


@functools.lru_cache(None)
def tables():
    out = {}
    c, s = turn(np.arange(8), np.arange(8), 8)
    eye = np.eye(32)
    out["row_one"] = two_parts(np.concatenate([np.kron(c, eye), np.kron(-s, eye)]))
    c, s = turn(np.arange(128), np.arange(512), 512)
    real = np.concatenate([c, s], axis=1)
    imag = np.concatenate([-s, c], axis=1)
    out["row_two"] = two_parts(np.stack([real, imag], axis=1).reshape(256, 1024))
    c, s = turn(np.arange(128), np.arange(128), 128)
    real = np.stack([c, s], axis=2).reshape(128, 256)
    imag = np.stack([-s, c], axis=2).reshape(128, 256)
    out["col_one"] = two_parts(np.concatenate([real, imag]))
    c, s = turn(np.arange(128), np.arange(32), NPIX)
    out["col_twist"] = np.stack([np.tile(c, (1, 4)), np.tile(s, (1, 4))]).astype(np.float32)
    c, s = turn(np.arange(32), np.arange(32), 32)
    same = np.eye(4)

    def spread(matrix):
        return np.einsum("tm,kl->tklm", matrix, same).reshape(128, 128)

    out["col_two"] = two_parts(np.block([[spread(c), spread(s)], [spread(-s), spread(c)]]))
    c, s = turn(np.arange(256), np.arange(256), 256)
    both = np.stack([c, -s]).reshape(2, NZ, NQ, 2, 256).transpose(2, 1, 0, 3, 4)
    out["box_one"] = two_parts(both.reshape(512, 256))
    c, s = turn(np.arange(32), np.arange(32), 32)
    out["box_two"] = two_parts(np.block([[c, s], [-s, c]]))
    return out


def halves(value):
    high = value.astype(bf16)
    return high, (value - high.astype(f32)).astype(bf16)


def mm(left, right):
    return lax.dot_general(left, right, (((1,), (0,)), ((), ())), preferred_element_type=f32)


def mmt(left, right):
    return lax.dot_general(left, right, (((1,), (1,)), ((), ())), preferred_element_type=f32)


def exact_product(table_ref, value, dot):
    return dot(table_ref[0], value) + dot(table_ref[1], value)


def full_product(table_ref, value, dot):
    high, low = halves(value)
    return dot(table_ref[0], high) + (dot(table_ref[1], high) + dot(table_ref[0], low))


def place():
    rows = lax.axis_index("rows")
    half = lax.axis_index("half")
    z = rows // NQ
    q = rows - z * NQ
    return rows, half, z, q, q * NY + half


def signal(barrier, rows, half):
    pl.semaphore_signal(barrier, inc=1, device_id=(rows, half), device_id_type=MESH)


def remote(src, dst, send, recv, rows, half):
    return pltpu.make_async_remote_copy(
        src_ref=src, dst_ref=dst, send_sem=send, recv_sem=recv, device_id=(rows, half), device_id_type=MESH
    )


def wait_for(ref, sem):
    pltpu.make_async_copy(ref, ref, sem).wait()


def loop(count, body, start=0):
    def step(index, carry):
        body(index)
        return carry

    lax.fori_loop(start, count, step, 0)


def gather_kernel(mic_ref, shift_ref, band_ref, table_ref, local, send, recv):
    rows, y, z, q, p = place()
    before, after = lax.rem(z + NZ - 1, NZ), lax.rem(z + 1, NZ)
    barrier = pltpu.get_barrier_semaphore()

    def greet(k):
        other = lax.rem(p + k, 32)
        signal(barrier, z * NQ + other // NY, lax.rem(other, NY))

    def greet_before(k):
        signal(barrier, before * NQ + k // NY, lax.rem(k, NY))

    loop(32, greet, 1)
    loop(32, greet_before)
    pl.semaphore_wait(barrier, 63)

    own = []
    for k in range(1, NY):
        for a in range(4):
            remote(
                mic_ref.at[:, pl.ds(256 * a, 256)], band_ref.at[NY * y + a], send.at[0], recv.at[0], rows, lax.rem(y + k, NY)
            ).start()
    for a in range(4):
        own.append(pltpu.make_async_copy(mic_ref.at[:, pl.ds(256 * a, 256)], band_ref.at[NY * y + a], local.at[a]))
    own.append(pltpu.make_async_copy(shift_ref, table_ref.at[p], local.at[4]))
    for copy in own:
        copy.start()

    def tell(k):
        other = lax.rem(p + k, 32)
        remote(shift_ref, table_ref.at[p], send.at[1], recv.at[1], z * NQ + other // NY, lax.rem(other, NY)).start()

    def tell_after(k):
        remote(shift_ref, table_ref.at[32 + p], send.at[1], recv.at[1], after * NQ + k // NY, lax.rem(k, NY)).start()

    loop(32, tell, 1)
    loop(32, tell_after)
    for copy in own:
        copy.wait()
    wait_for(band_ref.at[pl.ds(0, 12)], send.at[0])
    wait_for(band_ref.at[pl.ds(0, 12)], recv.at[0])
    wait_for(table_ref.at[pl.ds(0, 63)], send.at[1])
    wait_for(table_ref.at[pl.ds(0, 63)], recv.at[1])


def cut_kernel(where_ref, left_ref, table_ref, band_ref, boxes_ref, strip):
    q, y = where_ref[0], where_ref[1]
    lane = lax.broadcasted_iota(jnp.int32, (32, 256), 1)

    def one_band(d):
        near = q - d
        entry = jnp.where(near >= 0, near * NY + y, 32 + (near + NQ) * NY + y)
        for s in range(4):
            left = left_ref[d * 4 + s]
            block = left >> 8
            offset = left & 255
            first = band_ref[block].astype(f32)
            second = band_ref[jnp.minimum(block + 1, 15)].astype(f32)
            picked = jnp.where(lane >= offset, first, second)
            shift = (table_ref[entry, 0, 2 * s + 1] - offset) & 255
            strip[pl.ds(32 * s, 32), :] = pltpu.roll(picked, shift, 1)
        boxes_ref[:, d] = strip[...].T.reshape(32, 8, 128).astype(bf16)

    loop(REACH, one_band)


def row_kernel(band_ref, cos_ref, sin_ref, one_ref, two_ref, out_ref):
    real, imag = [], []
    for side in range(2):
        pixels = band_ref[:, side].reshape(256, 256)
        section = exact_product(one_ref, pixels, mm)
        cos = jnp.broadcast_to(cos_ref[:, 256 * side : 256 * side + 256][:, None, :], (8, 32, 256)).reshape(256, 256)
        sin = jnp.broadcast_to(sin_ref[:, 256 * side : 256 * side + 256][:, None, :], (8, 32, 256)).reshape(256, 256)
        real.append(section[:256] * cos + section[256:] * sin)
        imag.append(section[256:] * cos - section[:256] * sin)
    turned = jnp.concatenate(real + imag, axis=1)
    result = full_product(two_ref, turned, mmt).astype(bf16)
    out_ref[0] = result[:, :128]
    out_ref[1] = result[:, 128:]


def spread_kernel(freq_ref, boxes_ref, freq_out, boxes_out, local, send, recv):
    rows, y, z, q, p = place()
    before, after = lax.rem(z + NZ - 1, NZ), lax.rem(z + 1, NZ)
    barrier = pltpu.get_barrier_semaphore()

    def greet_rows(k):
        signal(barrier, lax.rem(rows + k, NBAND), y)

    def greet(k):
        other = lax.rem(p + k, 32)
        signal(barrier, z * NQ + other // NY, lax.rem(other, NY))

    def greet_after(k):
        signal(barrier, after * NQ + k // NY, lax.rem(k, NY))

    loop(NBAND, greet_rows, 1)
    loop(32, greet, 1)
    loop(32, greet_after)
    pl.semaphore_wait(barrier, NBAND - 1 + 63)

    def send_rows(k):
        other = lax.rem(rows + k, NBAND)
        remote(freq_ref.at[:, other], freq_out.at[:, rows], send.at[0], recv.at[0], other, y).start()

    here = p * REACH
    own_freq = pltpu.make_async_copy(freq_ref.at[:, rows], freq_out.at[:, rows], local.at[0])
    own_freq.start()

    for level in range(NQ):

        @pl.when(q == level)
        def _():
            near, far = level + 1, REACH - 1 - level

            def send_far(k):
                remote(
                    boxes_ref.at[pl.ds(k * REACH + near, far)],
                    boxes_out.at[pl.ds(here + near, far)],
                    send.at[2],
                    recv.at[2],
                    before * NQ + k // NY,
                    lax.rem(k, NY),
                ).start()

            def send_near(k):
                other = lax.rem(p + k, 32)
                remote(
                    boxes_ref.at[pl.ds(other * REACH, near)],
                    boxes_out.at[pl.ds(here, near)],
                    send.at[1],
                    recv.at[1],
                    z * NQ + other // NY,
                    lax.rem(other, NY),
                ).start()

            loop(32, send_far)
            loop(32, send_near, 1)
            own = pltpu.make_async_copy(boxes_ref.at[pl.ds(here, near)], boxes_out.at[pl.ds(here, near)], local.at[1])
            own.start()
            loop(NBAND, send_rows, 1)
            own.wait()
            wait_for(boxes_ref.at[pl.ds(0, 32 * far)], send.at[2])
            wait_for(boxes_ref.at[pl.ds(0, 31 * near)], send.at[1])
            wait_for(boxes_out.at[pl.ds(0, 144 - near)], recv.at[1])

    wait_for(boxes_out.at[pl.ds(0, 144)], recv.at[2])
    own_freq.wait()
    wait_for(freq_out.at[:, pl.ds(0, NBAND - 1)], send.at[0])
    wait_for(freq_out.at[:, pl.ds(0, NBAND - 1)], recv.at[0])


def class_kernel(top_ref, label_ref, table_ref, boxes_ref, one_ref, out_ref, acc):
    acc[...] = jnp.zeros_like(acc)
    lane = lax.broadcasted_iota(jnp.int32, (8, 128), 1)
    group = lane >> 5

    def one_home(home):
        q0 = home >> 2
        j = home & 3
        spun = []
        for d in range(REACH):
            piece = boxes_ref[(((q0 + d) & 7) * NY + j) * REACH + d].astype(f32)
            spun.append([piece] + [pltpu.roll(piece, 32 * turns, 1) for turns in range(1, 4)])

        def joined(first, s):
            value = spun[first][(0 - s) % 4]
            for dd in range(1, 4):
                value = jnp.where(group == dd, spun[first + dd][(dd - s) % 4], value)
            return value

        for s in range(4):
            slot = home * 4 + s
            top = top_ref[slot]
            shift = (table_ref[home, 0, 2 * s] - top) & 255
            low = jnp.where(lane >= top, joined(0, s), spun[8][(0 - s) % 4])
            box = pltpu.roll(jnp.concatenate([low, joined(4, s)], axis=1), shift, 1)
            label = label_ref[slot]
            acc[label] = acc[label] + box

    loop(32, one_home)
    main = full_product(one_ref, acc[0:48].reshape(384, 256), mmt).astype(bf16)
    for q in range(NQ):
        for t in range(3):
            out_ref[3 * q + t] = main[64 * q : 64 * q + 64, 128 * t : 128 * t + 128]
    rest = full_product(one_ref, acc[48:50].reshape(16, 256), mmt)
    rest = jnp.concatenate([rest[64 * q : 64 * q + 64] for q in range(NQ)], axis=1)
    out_ref[24] = rest.astype(bf16)


def sum_kernel(send_ref, got_ref, landed, sums, local, send, recv):
    rows, y, z, q, p = place()
    barrier = pltpu.get_barrier_semaphore()

    def greet_z(k):
        signal(barrier, lax.rem(z + k, NZ) * NQ + q, y)

    def greet(k):
        other = lax.rem(p + k, 32)
        signal(barrier, z * NQ + other // NY, lax.rem(other, NY))

    loop(NZ, greet_z, 1)
    loop(32, greet, 1)
    pl.semaphore_wait(barrier, 15 + 31)

    def send_z(k):
        other = lax.rem(z + k, NZ)
        remote(send_ref.at[:, other], landed.at[:, z], send.at[0], recv.at[0], other * NQ + q, y).start()

    loop(NZ, send_z, 1)
    own = pltpu.make_async_copy(send_ref.at[:, z], landed.at[:, z], local.at[0])
    own.start()
    own.wait()
    wait_for(landed.at[:, pl.ds(0, 15)], send.at[0])
    wait_for(landed.at[:, pl.ds(0, 15)], recv.at[0])
    for block in range(25):
        sums[block] = jnp.sum(landed[block].astype(f32), axis=0)

    def send_plane(k):
        other = lax.rem(p + k, 32)
        there = other // NY
        target = (z * NQ + there, lax.rem(other, NY))
        remote(sums.at[pl.ds(3 * there, 3)], got_ref.at[p, pl.ds(0, 3)], send.at[1], recv.at[1], *target).start()
        remote(sums.at[24], got_ref.at[p, 3], send.at[2], recv.at[2], *target).start()

    loop(32, send_plane, 1)
    mine = [
        pltpu.make_async_copy(sums.at[pl.ds(3 * q, 3)], got_ref.at[p, pl.ds(0, 3)], local.at[1]),
        pltpu.make_async_copy(sums.at[24], got_ref.at[p, 3], local.at[2]),
    ]
    for copy in mine:
        copy.start()
    for copy in mine:
        copy.wait()
    for index, count in ((1, 3), (2, 1)):
        wait_for(got_ref.at[pl.ds(0, 31), pl.ds(0, count)], send.at[index])
        wait_for(got_ref.at[pl.ds(0, 31), pl.ds(0, count)], recv.at[index])


def mean_kernel(where_ref, sums_ref, cos_ref, sin_ref, inverse_ref, two_ref, out_ref):
    q = where_ref[0]
    pieces = []
    for t in range(4):
        for a in range(2):
            pieces.append(jnp.concatenate([sums_ref[:, 4 * t + a, :], sums_ref[:, 4 * t + 2 + a, :]], axis=0))
    section = full_product(two_ref, jnp.concatenate(pieces, axis=1), mm)
    cos, sin = cos_ref[...], sin_ref[...]
    pattern = lax.broadcasted_iota(jnp.int32, (16, 128), 1) >> 3
    kind = lax.broadcasted_iota(jnp.int32, (16, 128), 0)
    for t in range(4):
        pick = (pattern == (kind if t < 3 else kind + 2 * q)).astype(bf16)
        for a in range(2):
            at = 128 * (2 * t + a)
            real = jnp.concatenate([section[:32, at : at + 128]] * 2, axis=0)
            imag = jnp.concatenate([section[32:, at : at + 128]] * 2, axis=0)
            for part, value in enumerate((real * cos + imag * sin, imag * cos - real * sin)):
                high, low = halves(value)
                total = mmt(pick, high) + mmt(pick, low)
                if t < 3:
                    out_ref[16 * t : 16 * t + 16, part, a, :] = total * inverse_ref[16 * t : 16 * t + 16]
                else:
                    out_ref[48:50, part, a, :] = total[:2] * inverse_ref[48:50]


def column_kernel(freq_ref, one_ref, twist_ref, two_ref, out_ref):
    cos, sin = twist_ref[0], twist_ref[1]
    for h in range(2):
        section = exact_product(one_ref, freq_ref[h], mm)
        real = section[:128] * cos + section[128:] * sin
        imag = section[128:] * cos - section[:128] * sin
        result = full_product(two_ref, jnp.concatenate([real, imag], axis=1), mmt)
        power = (result[:128] * result[:128] + result[128:] * result[128:]) * (1.0 / (NPIX * NPIX))
        for tau in range(32):
            out_ref[0, 4 * h : 4 * h + 4, 128 * tau : 128 * tau + 128] = power[4 * tau : 4 * tau + 4]


def call(kernel, outs, ins, out_specs, scratch=(), collective=None, name=None):
    params = dict(has_side_effects=True, collective_id=collective) if collective is not None else {}
    return pl.pallas_call(
        kernel,
        out_shape=outs,
        in_specs=ins,
        out_specs=out_specs,
        scratch_shapes=list(scratch),
        compiler_params=pltpu.CompilerParams(**params),
        name=name,
    )


def shape(*dims, dtype=bf16):
    return jax.ShapeDtypeStruct(dims, dtype)


def sems(count):
    return pltpu.SemaphoreType.DMA((count,))


def per_device(micrograph, box_tops, box_live, box_class, box_shift):
    consts = {name: jnp.asarray(value) for name, value in tables().items()}
    rows = lax.axis_index("rows")
    y = lax.axis_index("half")
    z = rows // NQ
    q = rows - z * NQ
    where = jnp.stack([q, y]).astype(jnp.int32)

    shifts = jnp.pad(box_shift.reshape(1, 8), ((0, 0), (0, 120)))
    band, table = call(
        gather_kernel,
        (shape(16, 32, 256), shape(64, 1, 128, dtype=jnp.int32)),
        [ANY, VMEM],
        (VMEM, VMEM),
        (sems(5), sems(2), sems(2)),
        collective=0,
        name="gather",
    )(micrograph, shifts)

    homes = jnp.mod(rows - jnp.arange(REACH, dtype=jnp.int32), NBAND)
    lefts = box_tops[homes, y, :, 1].reshape(-1)
    boxes = call(
        cut_kernel,
        shape(32, REACH, 8, 128),
        [SMEM, SMEM, SMEM, VMEM],
        VMEM,
        (pltpu.VMEM((128, 256), f32),),
        name="cut",
    )(where, lefts, table, band)

    octant = jnp.arange(8, dtype=jnp.int32)[:, None]
    column = jnp.arange(512, dtype=jnp.int32)[None, :]
    angles = (2.0 * np.pi / NPIX) * jnp.mod(column * (octant + 1024 * y), NPIX).astype(f32)
    freq = call(row_kernel, shape(2, 256, 128), [VMEM] * 5, VMEM, name="row")(
        band.reshape(8, 2, 32, 256), jnp.cos(angles), jnp.sin(angles), consts["row_one"], consts["row_two"]
    )

    freq, boxes = call(
        spread_kernel,
        (shape(2, NBAND, 2, 128), shape(32 * REACH, 8, 128)),
        [VMEM, VMEM],
        (VMEM, VMEM),
        (sems(2), sems(3), sems(3)),
        collective=1,
        name="spread",
    )(freq.reshape(2, NBAND, 2, 128), boxes.reshape(32 * REACH, 8, 128))

    plane_tops = lax.dynamic_slice_in_dim(box_tops[..., 0], z * NQ, NQ, 0)
    band_tops = (z * NQ + jnp.arange(NQ, dtype=jnp.int32)) * 32
    tops = (plane_tops - band_tops[:, None, None]).reshape(-1)
    plane_class = lax.dynamic_slice_in_dim(jnp.where(box_live == 1, box_class, CLASSES), z * NQ, NQ, 0)
    labels = plane_class.reshape(-1)
    to_z = call(
        class_kernel,
        shape(25, 64, 128),
        [SMEM, SMEM, SMEM, VMEM, VMEM],
        VMEM,
        (pltpu.VMEM((CLASSES + 1, 8, 256), f32),),
        name="classes",
    )(tops, labels, table, boxes, consts["box_one"])

    sums = call(
        sum_kernel,
        shape(32, 4, 4, 128, dtype=f32),
        [VMEM],
        VMEM,
        (pltpu.VMEM((25, NZ, 4, 128), bf16), pltpu.VMEM((25, 4, 128), f32), sems(3), sems(3), sems(3)),
        collective=2,
        name="sums",
    )(to_z.reshape(25, NZ, 4, 128))

    power = call(column_kernel, shape(1, 8, NPIX, dtype=f32), [VMEM] * 4, VMEM, name="column")(
        freq.reshape(2, 256, 128), consts["col_one"], consts["col_twist"], consts["col_two"]
    )

    kinds = jnp.arange(CLASSES, dtype=jnp.int32)[:, None, None, None]
    counts = jnp.sum(((box_class[None] == kinds) & (box_live[None] == 1)).astype(jnp.int32), axis=(1, 2, 3))
    inverse = (1.0 / (BOX * jnp.maximum(counts, 1).astype(f32)))[:, None]
    beta = jnp.arange(64, dtype=jnp.int32)[:, None] + 64 * y
    inner = jnp.arange(128, dtype=jnp.int32)[None, :] & 7
    angles = (2.0 * np.pi / BOX) * jnp.mod(beta * inner, BOX).astype(f32)
    means = call(
        mean_kernel, shape(CLASSES, 2, 2, 64, dtype=f32), [SMEM] + [VMEM] * 5, VMEM, name="means"
    )(where, sums.reshape(32, 16, 128), jnp.cos(angles), jnp.sin(angles), inverse, consts["box_two"])
    return power, means


def solution(mesh):
    in_specs = (P("rows", "half"), P(), P(), P(), P("rows", "half", None, None))
    out_specs = (P("half", "rows", None), P(None, None, "rows", "half"))
    return jax.shard_map(per_device, mesh=mesh, in_specs=in_specs, out_specs=out_specs, check_vma=False)
```

time: 251 us -> 124 us (0.49); the launches traced: 247 us -> 123 us
  Pallas kernels: 0 us -> 113 us
  waiting for transfers between devices: 72.2 us -> 0 us
  starting transfers between devices: 65.1 us -> 0 us
  matrix products: 63.4 us -> 0 us
  local copies, waits for them, and re-layouts: 36.7 us -> 5.3 us
  other arithmetic: 8.04 us -> 3.82 us
    pallas_call x0 -> x8, Pallas kernels: none -> 113 us  [the longest x1 39.8 us: per_device(): call(sum_kernel, shape(32, 4, 4, 128, dtype=f32), [VMEM], VMEM, (pltpu.VM...]
    dot_general x39 -> x0, matrix products: 63.4 us -> none  [the longest x14 17.8 us: product(): return jnp.einsum(pattern, left_side, matrix, precision=highest)]
    all_to_all x4 -> x0, waiting for transfers between devices: 50.8 us -> none  [the longest x1 42.2 us: per_device(): lax.all_to_all(spectra, 'rows', split_axis=2, concat_axis=0, tiled=True)]
    all_to_all x4 -> x0, starting transfers between devices: 47.6 us -> none  [the longest x1 23.4 us: per_device(): lax.all_to_all(partial_value, 'rows', split_axis=1, concat_axis=2, tiled=...]
    ppermute x8 -> x0, waiting for transfers between devices: 21.4 us -> none  [passed_along(): return lax.ppermute(block, axis, route)]
    ppermute x8 -> x0, starting transfers between devices: 17.5 us -> none  [passed_along(): return lax.ppermute(block, axis, route)]
    gather x12 -> x1, local copies, waits for them, and re-layouts: 10.4 us -> 0.67 us  [per_device(): lefts = box_tops[homes, y, :, 1].reshape(-1)]
    unnamed x23 -> x10, local copies, waits for them, and re-layouts: 9.1 us -> 0.8 us
  transfers between devices with their start and end apart: 12 -> 0, of which waited for: 6 -> 0; matrix products, arithmetic and copies ran while one was open for 40% -> 0% of each run, Pallas kernels for 0% -> 0%
where the time goes in v1:
time: 124 us; the launch traced here: 123 us
  Pallas kernels  113 us (91%)
  local copies, waits for them, and re-layouts  5.3 us (4%)
  other arithmetic  3.82 us (3%)
    pallas_call x1, Pallas kernels, per_device(): call(sum_kernel, shape(32, 4, 4, 128, dtype=f32), [VMEM], VMEM, (pltpu.VM...  39.8 us
    pallas_call x1, Pallas kernels, per_device(): call(spread_kernel, (shape(2, NBAND, 2, 128), shape(32 * REACH, 8, 128)),...  31.4 us
    pallas_call x1, Pallas kernels, per_device(): call(gather_kernel, (shape(16, 32, 256), shape(64, 1, 128, dtype=jnp.int3...  21.9 us
    pallas_call x1, Pallas kernels, per_device(): call(class_kernel, shape(25, 64, 128), [SMEM, SMEM, SMEM, VMEM, VMEM], VM...  8.19 us
    pallas_call x1, Pallas kernels, per_device(): call(cut_kernel, shape(32, REACH, 8, 128), [SMEM, SMEM, SMEM, VMEM], VMEM...  3.64 us
    pallas_call x1, Pallas kernels, per_device(): call(row_kernel, shape(2, 256, 128), [VMEM] * 5, VMEM, name='row')  3.61 us

profile of v1, /device:TPU:1, one launch (start us, length us, event | category | flops | bytes accessed | tf_op | source)
XLA Modules:
  0.0 123.3 jit_solution(13568586930842756579)
XLA Ops:
  0.7 0.6 pad_add_fusion.where_ref
  1.4 0.4 copy.29
  1.7 0.7 gather_fusion
  2.4 0.6 reshape.133.left_ref
  3.3 0.5 pad.4.shift_ref
  3.8 21.9 %gather.6 = (bf16[16,32,256]{2,1,0:T(8,128)(2,1)}, s32[64,1,128]{2,1,0:T(1,128)}) custom-call(bf16[32,1024]{1,0:T(8,128)(2,1)} %mic_ref.1, s32[1,128]{1,0:T(1,128)} %pad.4.shift_ref), custom_call_target="tpu_custom_call" | custom-call | tf_op jit(solution)/shard_map/gather/pallas_call | solution.py:424
  25.7 3.6 %cut.1 = bf16[32,9,8,128]{3,2,1,0:T(8,128)(2,1)} custom-call(s32[2]{0:T(128)} %pad_add_fusion.where_ref, s32[36]{0:T(128)} %reshape.133.left_ref, s32[64,1,128]{2,1,0:T(1,128)} %get-tuple-element.7.table_ref, bf16[16,32,256]{2,1,0:T(8,128)(2,1)} %get-tuple-element.6.band_ref), custom_call_target="tpu_custom_call" | custom-call | tf_op jit(solution)/shard_map/cut/pallas_call | solution.py:436
  29.3 0.8 fusion.12
  30.1 3.6 %row.1 = bf16[2,256,128]{2,1,0:T(8,128)(2,1)} custom-call(bf16[8,2,32,256]{3,2,1,0:T(8,128)(2,1)} %bitcast.16, f32[8,512]{1,0:T(8,128)} %get-tuple-element.13.cos_ref, f32[8,512]{1,0:T(8,128)} %get-tuple-element.12.sin_ref, bf16[2,512,256]{2,1,0:T(8,128)(2,1)} %constant.109.clone.one_ref, bf16[2,256,1024]{2,1,0:T(8,128)(2,1)} %constant.110.clone.two_ref), custom_call_target="tpu_custom_call" | custom-call | tf_op jit(solution)/shard_map/row/pallas_call | solution.py:448
  33.7 31.4 %spread.1 = (bf16[2,128,2,128]{3,2,1,0:T(2,128)(2,1)}, bf16[288,8,128]{2,1,0:T(8,128)(2,1)}) custom-call(bf16[2,128,2,128]{3,2,1,0:T(2,128)(2,1)} %bitcast.18, bf16[288,8,128]{2,1,0:T(8,128)(2,1)} %bitcast.14), custom_call_target="tpu_custom_call" | custom-call | tf_op jit(solution)/shard_map/spread/pallas_call | solution.py:452
  65.1 0.7 slice-done
  65.9 0.1 copy.30
  66.0 0.1 dynamic_slice.9
  66.2 0.1 sub.36
  66.3 0.5 sub.37.top_ref
  66.9 0.1 copy-done.1
  67.2 0.6 reshape.136.label_ref
  67.8 8.2 %classes.1 = bf16[25,64,128]{2,1,0:T(8,128)(2,1)} custom-call(s32[128]{0:T(128)} %sub.37.top_ref, s32[128]{0:T(128)} %reshape.136.label_ref, s32[64,1,128]{2,1,0:T(1,128)} %get-tuple-element.7.table_ref, bf16[288,8,128]{2,1,0:T(8,128)(2,1)} %get-tuple-element.9.boxes_ref, bf16[2,512,256]{2,1,0:T(8,128)(2,1)} %constant.114.clone.one_ref), custom_call_target="tpu_custom_call" | custom-call | tf_op jit(solution)/shard_map/classes/pallas_call | solution.py:467
  76.0 39.8 %sums.1 = f32[32,4,4,128]{3,2,1,0:T(4,128)} custom-call(bf16[25,16,4,128]{3,2,1,0:T(4,128)(2,1)} %bitcast.15), custom_call_target="tpu_custom_call" | custom-call | tf_op jit(solution)/shard_map/sums/pallas_call | solution.py:476
  115.8 0.8 fusion.7
  116.7 1.0 convert_reduce_fusion
  117.7 0.7 copy.32.inverse_ref
  118.4 2.4 %means.1 = f32[50,2,2,64]{3,2,1,0:T(2,128)} custom-call(s32[2]{0:T(128)} %pad_add_fusion.where_ref, f32[32,16,128]{2,1,0:T(8,128)} %bitcast.17, f32[64,128]{1,0:T(8,128)} %get-tuple-element.11.cos_ref, f32[64,128]{1,0:T(8,128)} %get-tuple-element.10.sin_ref, f32[50,1]{1,0:T(8,128)} %copy.32.inverse_ref, bf16[2,64,64]{2,1,0:T(8,128)(2,1)} %constant.115.clone.two_ref), custom_call_target="tpu_custom_call" | custom-call | tf_op jit(solution)/shard_map/means/pallas_call | solution.py:496
  120.8 2.5 %column.1 = f32[1,8,4096]{2,1,0:T(8,128)} custom-call(bf16[2,256,128]{2,1,0:T(8,128)(2,1)} %bitcast.19, bf16[2,256,256]{2,1,0:T(8,128)(2,1)} %constant.111.clone.one_ref, f32[2,128,128]{2,1,0:T(8,128)} %constant.112.clone.twist_ref, bf16[2,256,256]{2,1,0:T(8,128)(2,1)} %constant.113.clone.two_ref), custom_call_target="tpu_custom_call" | custom-call | tf_op jit(solution)/shard_map/column/pallas_call | solution.py:486
  (21 shorter events, 0.8 us)
Async XLA Ops:
  0.6 0.7 copy-start
  2.4 0.7 copy-start.3
  65.1 0.7 slice-start
  66.2 0.7 copy-start.2
  66.3 0.7 copy-start.1

commit v2 on v1

v2 whole, which is shorter than its diff:
```python
import functools

import jax
import jax.numpy as jnp
import numpy as np
from jax import lax
from jax.experimental import pallas as pl
from jax.experimental.pallas import tpu as pltpu
from jax.sharding import PartitionSpec as P

BOX = 256
CLASSES = 50
NPIX = 4096
NZ, NQ, NY = 16, 8, 4
NBAND = 128
REACH = 9
MESH = pl.DeviceIdType.MESH
f32 = jnp.float32
bf16 = jnp.bfloat16
VMEM = pl.BlockSpec(memory_space=pltpu.VMEM)
SMEM = pl.BlockSpec(memory_space=pltpu.SMEM)
ANY = pl.BlockSpec(memory_space=pl.ANY)


def two_parts(matrix):
    high = matrix.astype(bf16)
    return np.stack([high, (matrix - high.astype(np.float64)).astype(bf16)])


def turn(left, right, length):
    angle = 2.0 * np.pi / length * np.mod(np.multiply.outer(left, right), length)
    return np.cos(angle), np.sin(angle)


@functools.lru_cache(None)
def tables():
    out = {}
    c, s = turn(np.arange(8), np.arange(8), 8)
    eye = np.eye(32)
    out["row_one"] = two_parts(np.concatenate([np.kron(c, eye), np.kron(-s, eye)]))
    angle = np.arange(8)[None] + 1024 * np.arange(4)[:, None]
    c, s = turn(angle, np.arange(512), NPIX)
    out["row_twist"] = np.stack([c, s], axis=1).astype(np.float32)
    c, s = turn(np.arange(128), np.arange(512), 512)
    real = np.concatenate([c, s], axis=1)
    imag = np.concatenate([-s, c], axis=1)
    out["row_two"] = two_parts(np.stack([real, imag], axis=1).reshape(256, 1024))
    c, s = turn(np.arange(128), np.arange(128), 128)
    real = np.stack([c, s], axis=2)
    imag = np.stack([-s, c], axis=2)
    both = np.concatenate([real, imag]).reshape(256, NZ, NQ, 2).transpose(0, 2, 1, 3)
    out["col_one"] = two_parts(both.reshape(256, 256))
    c, s = turn(np.arange(128), np.arange(32), NPIX)
    out["col_twist"] = np.stack([np.tile(c, (1, 4)), np.tile(s, (1, 4))]).astype(np.float32)
    c, s = turn(np.arange(32), np.arange(32), 32)
    same = np.eye(4)

    def spread(matrix):
        return np.einsum("tm,kl->tklm", matrix, same).reshape(128, 128)

    out["col_two"] = two_parts(np.block([[spread(c), spread(s)], [spread(-s), spread(c)]]))
    c, s = turn(np.arange(256), np.arange(256), 256)
    both = np.stack([c, -s]).reshape(2, NZ, NQ, 2, 256).transpose(2, 1, 0, 3, 4)
    out["box_one"] = two_parts(both.reshape(512, 256))
    c, s = turn(np.arange(32), np.arange(32), 32)
    out["box_two"] = two_parts(np.block([[c, s], [-s, c]]))
    lanes = np.concatenate([np.arange(384) // 48, (np.arange(128) >> 1) & 7])
    c, s = turn(np.arange(64), lanes, 256)
    out["box_twist"] = np.stack([c, s]).astype(np.float32)
    c, s = turn(np.arange(4), lanes, 4)
    out["box_quarter"] = np.stack([c, s], axis=1).reshape(4, 2, 512).astype(np.float32)
    return out


def halves(value):
    high = value.astype(bf16)
    return high, (value - high.astype(f32)).astype(bf16)


def mm(left, right):
    return lax.dot_general(left, right, (((1,), (0,)), ((), ())), preferred_element_type=f32)


def mmt(left, right):
    return lax.dot_general(left, right, (((1,), (1,)), ((), ())), preferred_element_type=f32)


def exact_product(table_ref, value, dot):
    return dot(table_ref[0], value) + dot(table_ref[1], value)


def full_product(table_ref, value, dot):
    high, low = halves(value)
    return dot(table_ref[0], high) + (dot(table_ref[1], high) + dot(table_ref[0], low))


def place():
    rows = lax.axis_index("rows")
    half = lax.axis_index("half")
    z = rows // NQ
    q = rows - z * NQ
    return rows, half, z, q, q * NY + half


def signal(barrier, rows, half):
    pl.semaphore_signal(barrier, inc=1, device_id=(rows, half), device_id_type=MESH)


def remote(src, dst, send, recv, rows, half):
    return pltpu.make_async_remote_copy(
        src_ref=src, dst_ref=dst, send_sem=send, recv_sem=recv, device_id=(rows, half), device_id_type=MESH
    )


def wait_for(ref, sem):
    pltpu.make_async_copy(ref, ref, sem).wait()


def loop(count, body, start=0):
    def step(index, carry):
        body(index)
        return carry

    lax.fori_loop(start, count, step, 0)


def signal_plane(barrier, z, p):
    def greet(k):
        other = lax.rem(p + k, 32)
        signal(barrier, z * NQ + other // NY, lax.rem(other, NY))

    loop(32, greet, 1)


def gather_kernel(mic_ref, shift_ref, band_ref, table_ref, local, send, recv):
    rows, y, z, q, p = place()
    before, after = lax.rem(z + NZ - 1, NZ), lax.rem(z + 1, NZ)
    own = []
    for a in range(4):
        own.append(pltpu.make_async_copy(mic_ref.at[:, pl.ds(256 * a, 256)], band_ref.at[NY * y + a], local.at[a]))
    own.append(pltpu.make_async_copy(shift_ref, table_ref.at[p], local.at[4]))
    for copy in own:
        copy.start()
    barrier = pltpu.get_barrier_semaphore()
    signal_plane(barrier, z, p)
    for k in range(NQ):
        signal(barrier, before * NQ + k, y)
    for copy in own:
        copy.wait()
    pl.semaphore_wait(barrier, 31 + NQ)

    mine = band_ref.at[pl.ds(NY * y, 4)]
    for k in range(1, NY):
        remote(mine, mine, send.at[0], recv.at[0], rows, lax.rem(y + k, NY)).start()
    for k in range(NQ):
        remote(table_ref.at[p], table_ref.at[32 + q], send.at[1], recv.at[1], after * NQ + k, y).start()

    def tell(k):
        other = lax.rem(p + k, 32)
        remote(
            table_ref.at[p], table_ref.at[p], send.at[1], recv.at[1], z * NQ + other // NY, lax.rem(other, NY)
        ).start()

    loop(32, tell, 1)
    wait_for(band_ref.at[pl.ds(0, 12)], send.at[0])
    wait_for(table_ref.at[pl.ds(0, 31 + NQ)], send.at[1])
    wait_for(band_ref.at[pl.ds(0, 12)], recv.at[0])
    wait_for(table_ref.at[pl.ds(0, 31 + NQ)], recv.at[1])


def spread_kernel(
    code_ref, table_ref, band_ref, twist_ref, one_hbm, two_hbm, freq_out, boxes_out,
    one_ref, two_ref, strip, boxes, freq, local, send, recv,
):
    rows, y, z, q, p = place()
    before, after = lax.rem(z + NZ - 1, NZ), lax.rem(z + 1, NZ)
    barrier = pltpu.get_barrier_semaphore()
    load_one = pltpu.make_async_copy(one_hbm, one_ref, local.at[0])
    load_two = pltpu.make_async_copy(two_hbm, two_ref, local.at[1])
    load_one.start()
    load_two.start()

    def greet_z(k):
        signal(barrier, lax.rem(z + k, NZ) * NQ + q, y)

    def greet_after(k):
        signal(barrier, after * NQ + k // NY, lax.rem(k, NY))

    loop(NZ, greet_z, 1)
    signal_plane(barrier, z, p)
    loop(32, greet_after)

    lane = lax.broadcasted_iota(jnp.int32, (32, 256), 1)

    def one_band(d):
        near = q - d
        entry = jnp.where(near >= 0, near * NY + y, 32 + near + NQ)
        home = lax.rem(rows - d + NBAND, NBAND)
        for s in range(4):
            left = (code_ref[home // NQ, lax.rem(home, NQ) * 16 + y * 4 + s] >> 12) & 4095
            block = left >> 8
            offset = left & 255
            first = band_ref[block].astype(f32)
            second = band_ref[jnp.minimum(block + 1, 15)].astype(f32)
            picked = jnp.where(lane >= offset, first, second)
            shift = (table_ref[entry, 0, 2 * s + 1] - offset) & 255
            strip[pl.ds(32 * s, 32), :] = pltpu.roll(picked, shift, 1)
        boxes[:, d] = strip[...].T.reshape(32, 8, 128).astype(bf16)

    loop(REACH, one_band)
    pl.semaphore_wait(barrier, 15 + 63)

    here = p
    for level in range(NQ):

        @pl.when(q == level)
        def _():
            near, far = level + 1, REACH - 1 - level

            def send_far(k):
                remote(
                    boxes.at[k, pl.ds(near, far)], boxes_out.at[pl.ds(here * REACH + near, far)],
                    send.at[2], recv.at[2], before * NQ + k // NY, lax.rem(k, NY),
                ).start()

            def send_near(k):
                other = lax.rem(p + k, 32)
                remote(
                    boxes.at[other, pl.ds(0, near)], boxes_out.at[pl.ds(here * REACH, near)],
                    send.at[1], recv.at[1], z * NQ + other // NY, lax.rem(other, NY),
                ).start()

            loop(32, send_far)
            loop(32, send_near, 1)
            pltpu.make_async_copy(boxes.at[here, pl.ds(0, near)], boxes_out.at[pl.ds(here * REACH, near)], local.at[2]).start()

    load_one.wait()
    load_two.wait()
    real, imag = [], []
    cos_all, sin_all = twist_ref[y, 0], twist_ref[y, 1]
    for side in range(2):
        pixels = band_ref[:, :].reshape(8, 2, 32, 256)[:, side].reshape(256, 256)
        section = exact_product(one_ref, pixels, mm)
        cos = jnp.broadcast_to(cos_all[:, 256 * side : 256 * side + 256][:, None, :], (8, 32, 256)).reshape(256, 256)
        sin = jnp.broadcast_to(sin_all[:, 256 * side : 256 * side + 256][:, None, :], (8, 32, 256)).reshape(256, 256)
        real.append(section[:256] * cos + section[256:] * sin)
        imag.append(section[256:] * cos - section[:256] * sin)
    turned = jnp.concatenate(real + imag, axis=1)
    result = full_product(two_ref, turned, mmt).astype(bf16)
    freq[0] = result[:, :128]
    freq[1] = result[:, 128:]

    def send_z(k):
        other = lax.rem(z + k, NZ)
        remote(
            freq.at[:, pl.ds(16 * other, 16)], freq_out.at[:, z], send.at[0], recv.at[0], other * NQ + q, y
        ).start()

    loop(NZ, send_z, 1)
    own = pltpu.make_async_copy(freq.at[:, pl.ds(16 * z, 16)], freq_out.at[:, z], local.at[3])
    own.start()

    for level in range(NQ):

        @pl.when(q == level)
        def _():
            near, far = level + 1, REACH - 1 - level
            wait_for(boxes.at[0, pl.ds(0, near)], local.at[2])
            wait_for(boxes.at[pl.ds(0, 32), pl.ds(0, far)], send.at[2])
            wait_for(boxes.at[pl.ds(0, 31), pl.ds(0, near)], send.at[1])
            wait_for(whole_pieces(boxes_out, 144 - near), recv.at[1])

    wait_for(whole_pieces(boxes_out, 144), recv.at[2])
    own.wait()
    wait_for(freq_out.at[:, pl.ds(0, 15)], send.at[0])
    wait_for(freq_out.at[:, pl.ds(0, 15)], recv.at[0])


def sum_kernel(
    code_ref, table_ref, labels_ref, boxes_ref, freq_ref, one_hbm, two_ref, twist_ref, quarter_ref, col_one_hbm, col_twist_ref,
    col_two_hbm, power_ref, means_ref, one_ref, col_one_ref, col_two_ref, held, to_z, landed, sums, got, freq, local, send, recv,
):
    rows, y, z, q, p = place()
    barrier = pltpu.get_barrier_semaphore()
    loads = [
        pltpu.make_async_copy(one_hbm, one_ref, local.at[4]),
        pltpu.make_async_copy(col_one_hbm, col_one_ref, local.at[5]),
        pltpu.make_async_copy(col_two_hbm, col_two_ref, local.at[6]),
    ]
    for load in loads:
        load.start()

    def greet_z(k):
        signal(barrier, lax.rem(z + k, NZ) * NQ + q, y)

    loop(NZ, greet_z, 1)
    signal_plane(barrier, z, p)

    lane = lax.broadcasted_iota(jnp.int32, (8, 128), 1)
    group = lane >> 5

    def one_home(home):
        q0 = home >> 2
        j = home & 3
        spun = []
        for d in range(REACH):
            piece = boxes_ref[(((q0 + d) & 7) * NY + j) * REACH + d].astype(f32)
            spun.append([piece] + [pltpu.roll(piece, 32 * turns, 1) for turns in range(1, 4)])

        def joined(first, s):
            value = spun[first][(0 - s) % 4]
            for dd in range(1, 4):
                value = jnp.where(group == dd, spun[first + dd][(dd - s) % 4], value)
            return value

        for s in range(4):
            slot = home * 4 + s
            top = ((code_ref[z, slot] & 4095) - rows_of(z, q0)) & 255
            shift = (table_ref[home, 0, 2 * s] - top) & 255
            low = jnp.where(lane >= top, joined(0, s), spun[8][(0 - s) % 4])
            held[slot] = pltpu.roll(jnp.concatenate([low, joined(4, s)], axis=1), shift, 1)

    loop(32, one_home)

    kinds = lax.broadcasted_iota(jnp.int32, (64, 128), 0)
    chosen = (kinds == (labels_ref[pl.ds(z, 1), :] >> 24)).astype(bf16)
    columns = [mm(chosen, held[:, c, :].astype(bf16)) for c in range(8)]
    loads[0].wait()
    main = full_product(one_ref, jnp.concatenate([column[:48] for column in columns], axis=0), mmt)
    rest = full_product(one_ref, jnp.concatenate([column[48:50] for column in columns], axis=0), mmt)
    rest = jnp.concatenate([rest[64 * k : 64 * k + 64] for k in range(NQ)], axis=1)
    for k in range(NQ):
        for t in range(3):
            to_z[3 * k + t] = main[64 * k : 64 * k + 64, 128 * t : 128 * t + 128].reshape(NZ, 4, 128).astype(bf16)
    to_z[24] = rest.reshape(NZ, 4, 128).astype(bf16)
    pl.semaphore_wait(barrier, 15 + 31)

    def send_z(k):
        other = lax.rem(z + k, NZ)
        remote(to_z.at[:, other], landed.at[:, z], send.at[0], recv.at[0], other * NQ + q, y).start()

    def send_q(k):
        other = lax.rem(q + k, NQ)
        remote(freq_ref.at[:, :, other], freq.at[:, q], send.at[2], recv.at[2], z * NQ + other, y).start()

    loop(NQ, send_q, 1)
    loop(NZ, send_z, 1)
    own = [
        pltpu.make_async_copy(to_z.at[:, z], landed.at[:, z], local.at[0]),
        pltpu.make_async_copy(freq_ref.at[:, :, q], freq.at[:, q], local.at[1]),
    ]
    for copy in own:
        copy.start()

    cos_y, sin_y = quarter_ref[y, 0][None, :], quarter_ref[y, 1][None, :]
    cos = twist_ref[0] * cos_y - twist_ref[1] * sin_y
    sin = twist_ref[1] * cos_y + twist_ref[0] * sin_y

    counts = jnp.zeros((64, 128), f32)
    for k in range(NZ):
        counts = counts + (kinds == (labels_ref[k : k + 1, :] >> 24)).astype(f32)
    inverse = 1.0 / (BOX * jnp.maximum(jnp.sum(counts, axis=1, keepdims=True), 1.0))

    for load in loads[1:]:
        load.wait()
    own[1].wait()
    wait_for(freq.at[:, pl.ds(0, NQ - 1)], send.at[2])
    wait_for(freq.at[:, pl.ds(0, NQ - 1)], recv.at[2])
    col_cos, col_sin = col_twist_ref[0], col_twist_ref[1]
    for h in range(2):
        section = exact_product(col_one_ref, freq[h].reshape(256, 128), mm)
        real = section[:128] * col_cos + section[128:] * col_sin
        imag = section[128:] * col_cos - section[:128] * col_sin
        result = full_product(col_two_ref, jnp.concatenate([real, imag], axis=1), mmt)
        power = (result[:128] * result[:128] + result[128:] * result[128:]) * (1.0 / (NPIX * NPIX))
        for tau in range(32):
            power_ref[0, 4 * h : 4 * h + 4, 128 * tau : 128 * tau + 128] = power[4 * tau : 4 * tau + 4]

    own[0].wait()
    wait_for(landed.at[:, pl.ds(0, 15)], send.at[0])
    wait_for(landed.at[:, pl.ds(0, 15)], recv.at[0])
    last = jnp.sum(landed[24].astype(f32), axis=0)
    for k in range(NQ):
        for t in range(3):
            sums[k, t] = jnp.sum(landed[3 * k + t].astype(f32), axis=0)
        sums[k, 3] = last

    def send_plane(k):
        other = lax.rem(p + k, 32)
        there = other // NY
        remote(sums.at[there], got.at[p], send.at[1], recv.at[1], z * NQ + there, lax.rem(other, NY)).start()

    loop(32, send_plane, 1)
    mine = pltpu.make_async_copy(sums.at[q], got.at[p], local.at[2])
    mine.start()
    mine.wait()
    wait_for(got.at[pl.ds(0, 31)], send.at[1])
    wait_for(got.at[pl.ds(0, 31)], recv.at[1])

    pieces = []
    for a in range(2):
        for t in range(4):
            pieces.append(jnp.concatenate([got[:, t, a, :], got[:, t, 2 + a, :]], axis=0))
    section = full_product(two_ref, jnp.concatenate(pieces, axis=1), mm)
    lanes = lax.broadcasted_iota(jnp.int32, (48, 384), 1)
    pick = (lax.rem(lanes, 48) == lax.broadcasted_iota(jnp.int32, (48, 384), 0)).astype(bf16)
    lanes = lax.broadcasted_iota(jnp.int32, (16, 128), 1)
    pick_rest = (((lanes >> 4) == q) & ((lanes & 1) == lax.broadcasted_iota(jnp.int32, (16, 128), 0))).astype(bf16)
    for a in range(2):
        real = jnp.concatenate([section[:32, 512 * a : 512 * a + 512]] * 2, axis=0)
        imag = jnp.concatenate([section[32:, 512 * a : 512 * a + 512]] * 2, axis=0)
        for part, value in enumerate((real * cos + imag * sin, imag * cos - real * sin)):
            high, low = halves(value)
            total = mmt(pick, high[:, :384]) + mmt(pick, low[:, :384])
            means_ref[0:48, part, a, :] = total * inverse[:48]
            total = mmt(pick_rest, high[:, 384:]) + mmt(pick_rest, low[:, 384:])
            means_ref[48:50, part, a, :] = total[:2] * inverse[48:50]


def rows_of(z, q0):
    return (z * NQ + q0) * 32


def whole_pieces(ref, count):
    return ref.at[pl.ds(0, count)]


def call(kernel, outs, ins, out_specs, scratch=(), collective=None, name=None):
    params = dict(has_side_effects=True, collective_id=collective) if collective is not None else {}
    return pl.pallas_call(
        kernel,
        out_shape=outs,
        in_specs=ins,
        out_specs=out_specs,
        scratch_shapes=list(scratch),
        compiler_params=pltpu.CompilerParams(**params),
        name=name,
    )


def shape(*dims, dtype=bf16):
    return jax.ShapeDtypeStruct(dims, dtype)


def sems(count):
    return pltpu.SemaphoreType.DMA((count,))


def per_device(micrograph, box_tops, box_live, box_class, box_shift):
    consts = {name: jnp.asarray(value) for name, value in tables().items()}
    labels = jnp.where(box_live == 1, box_class, CLASSES)
    codes = ((labels * 4096 + box_tops[..., 1]) * 4096 + box_tops[..., 0]).reshape(NZ, 128)

    shifts = jnp.pad(box_shift.reshape(1, 8), ((0, 0), (0, 120)))
    band, table = call(
        gather_kernel,
        (shape(16, 32, 256), shape(32 + NQ, 1, 128, dtype=jnp.int32)),
        [ANY, VMEM],
        (VMEM, VMEM),
        (sems(5), sems(2), sems(2)),
        collective=0,
        name="gather",
    )(micrograph, shifts)

    freq, boxes = call(
        spread_kernel,
        (shape(2, NZ, 16, 128), shape(32 * REACH, 8, 128)),
        [SMEM, SMEM, VMEM, VMEM, ANY, ANY],
        (VMEM, VMEM),
        (
            pltpu.VMEM((2, 512, 256), bf16),
            pltpu.VMEM((2, 256, 1024), bf16),
            pltpu.VMEM((128, 256), f32),
            pltpu.VMEM((32, REACH, 8, 128), bf16),
            pltpu.VMEM((2, 256, 128), bf16),
            sems(4),
            sems(3),
            sems(3),
        ),
        collective=1,
        name="spread",
    )(codes, table, band, consts["row_twist"], consts["row_one"], consts["row_two"])

    power, means = call(
        sum_kernel,
        (shape(1, 8, NPIX, dtype=f32), shape(CLASSES, 2, 2, 64, dtype=f32)),
        [SMEM, SMEM, VMEM, VMEM, VMEM, ANY, VMEM, VMEM, VMEM, ANY, VMEM, ANY],
        (VMEM, VMEM),
        (
            pltpu.VMEM((2, 512, 256), bf16),
            pltpu.VMEM((2, 256, 256), bf16),
            pltpu.VMEM((2, 256, 256), bf16),
            pltpu.VMEM((128, 8, 256), f32),
            pltpu.VMEM((25, NZ, 4, 128), bf16),
            pltpu.VMEM((25, NZ, 4, 128), bf16),
            pltpu.VMEM((NQ, 4, 4, 128), f32),
            pltpu.VMEM((32, 4, 4, 128), f32),
            pltpu.VMEM((2, NQ, NZ, 2, 128), bf16),
            sems(7),
            sems(3),
            sems(3),
        ),
        collective=2,
        name="sums",
    )(
        codes, table, codes, boxes, freq.reshape(2, NZ, NQ, 2, 128), consts["box_one"], consts["box_two"], consts["box_twist"],
        consts["box_quarter"], consts["col_one"], consts["col_twist"], consts["col_two"],
    )
    return power, means


def solution(mesh):
    in_specs = (P("rows", "half"), P(), P(), P(), P("rows", "half", None, None))
    out_specs = (P("half", "rows", None), P(None, None, "rows", "half"))
    return jax.shard_map(per_device, mesh=mesh, in_specs=in_specs, out_specs=out_specs, check_vma=False)
```

time: 124 us -> 91.8 us (0.74)
  Pallas kernels: 113 us -> 85.3 us
  other arithmetic: 3.82 us -> 0.01 us
    pallas_call x8 -> x3, Pallas kernels: 113 us -> 85.3 us  [the longest x1 40.4 us: per_device(): call(sum_kernel, (shape(1, 8, NPIX, dtype=f32), shape(CLASSES, 2, 2, 64,...]
    unnamed x10 -> x9, local copies, waits for them, and re-layouts: 0.8 us -> 3.02 us
    sin x2 -> x0, other arithmetic: 1.6 us -> none  [per_device(): jnp.sin(angles)]
where the time goes in v2:
time: 91.8 us; the launch traced here: 91.4 us
  Pallas kernels  85.3 us (93%)
  local copies, waits for them, and re-layouts  5.47 us (6%)
    pallas_call x1, Pallas kernels, per_device(): call(sum_kernel, (shape(1, 8, NPIX, dtype=f32), shape(CLASSES, 2, 2, 64,...  40.4 us
    pallas_call x1, Pallas kernels, per_device(): call(spread_kernel, (shape(2, NZ, 16, 128), shape(32 * REACH, 8, 128)), [...  24.4 us
    pallas_call x1, Pallas kernels, per_device(): call(gather_kernel, (shape(16, 32, 256), shape(32 + NQ, 1, 128, dtype=jnp...  20.5 us
    unnamed x9, local copies, waits for them, and re-layouts  3.02 us

profile of v2, /device:TPU:1, one launch (start us, length us, event | category | flops | bytes accessed | tf_op | source)
XLA Modules:
  0.0 91.4 jit_solution(11614151738555946171)
XLA Ops:
  0.6 0.8 copy.24
  1.4 0.1 reshape.14
  1.5 0.5 pad.4.shift_ref
  2.0 0.0 copy-start.1
  2.0 0.0 copy-start.2
  2.0 0.8 fusion
  2.8 0.0 copy-done.1
  2.8 0.0 copy-done.2
  2.9 0.2 copy.23
  3.0 0.9 reshape.13.code_ref.labels_ref
  3.9 20.5 %gather.1 = (bf16[16,32,256]{2,1,0:T(8,128)(2,1)}, s32[40,1,128]{2,1,0:T(1,128)}) custom-call(bf16[32,1024]{1,0:T(8,128)(2,1)} %mic_ref.1, s32[1,128]{1,0:T(1,128)} %pad.4.shift_ref), custom_call_target="tpu_custom_call" | custom-call | tf_op jit(solution)/shard_map/gather/pallas_call | solution.py:455
  24.4 24.4 %spread.1 = (bf16[2,16,16,128]{3,2,1,0:T(8,128)(2,1)}, bf16[288,8,128]{2,1,0:T(8,128)(2,1)}) custom-call(s32[16,128]{1,0:T(8,128)} %reshape.13.code_ref.labels_ref, s32[40,1,128]{2,1,0:T(1,128)} %get-tuple-element.6.table_ref, bf16[16,32,256]{2,1,0:T(8,128)(2,1)} %get-tuple-element.7.band_ref, f32[4,2,8,512]{3,2,1,0:T(8,128)} %constant.29.clone.twist_ref, ...), custom_call_target="tpu_custom_call" | custom-call | tf_op jit(solution)/shard_map/spread/pallas_call | solution.py:465
  48.8 40.4 %sums.1 = (f32[1,8,4096]{2,1,0:T(8,128)}, f32[50,2,2,64]{3,2,1,0:T(2,128)}) custom-call(s32[16,128]{1,0:T(8,128)} %reshape.13.code_ref.labels_ref, s32[40,1,128]{2,1,0:T(1,128)} %get-tuple-element.6.table_ref, s32[16,128]{1,0:T(8,128)} %reshape.13.code_ref.labels_ref, bf16[288,8,128]{2,1,0:T(8,128)(2,1)} %get-tuple-element.8.boxes_ref, ...), custom_call_target="tpu_custom_call" | custom-call | tf_op jit(solution)/shard_map/sums/pallas_call | solution.py:484
  89.2 0.0 copy-start
  89.2 1.6 %copy.29 = f32[1,8,4096]{2,1,0:T(8,128)} copy(f32[1,8,4096]{2,1,0:T(8,128)} %get-tuple-element.14) | data formatting | bytes 262144
  90.8 0.0 copy-done
  90.8 0.6 copy.30
  (1 shorter events, 0.0 us)
Async XLA Ops:
  2.0 0.8 copy-start.1
  2.0 0.8 copy-start.2
  89.2 1.6 %copy-start = (f32[50,2,2,64]{3,2,1,0:T(2,128)S(1)}, f32[50,2,2,64]{3,2,1,0:T(2,128)}, u32[]{:S(2)}) copy-start(f32[50,2,2,64]{3,2,1,0:T(2,128)} %get-tuple-element.15) | copy-start | bytes 153604

commit v3 on v2

--- a/solution.py
+++ b/solution.py
@@ -44,7 +44,8 @@
     c, s = turn(np.arange(128), np.arange(512), 512)
     real = np.concatenate([c, s], axis=1)
     imag = np.concatenate([-s, c], axis=1)
-    out["row_two"] = two_parts(np.stack([real, imag], axis=1).reshape(256, 1024))
+    both = np.stack([real, imag], axis=1).reshape(NZ, NQ, 2, 1024).transpose(1, 0, 2, 3)
+    out["row_two"] = two_parts(both.reshape(256, 1024))
     c, s = turn(np.arange(128), np.arange(128), 128)
     real = np.stack([c, s], axis=2)
     imag = np.stack([-s, c], axis=2)
@@ -168,27 +169,36 @@
     wait_for(table_ref.at[pl.ds(0, 31 + NQ)], recv.at[1])
 
 
-def spread_kernel(
-    code_ref, table_ref, band_ref, twist_ref, one_hbm, two_hbm, freq_out, boxes_out,
-    one_ref, two_ref, strip, boxes, freq, local, send, recv,
+def far_first(count):
+    return sorted(range(1, count), key=lambda k: -min(k, count - k))
+
+
+def main_kernel(
+    tops_ref, table_ref, class_ref, live_ref, band_ref, row_twist_ref, box_twist_ref, quarter_ref, col_twist_ref, box_two_ref,
+    row_one_hbm, row_two_hbm, box_one_hbm, col_one_hbm, col_two_hbm, power_ref, means_ref,
+    row_one_ref, row_two_ref, box_one_ref, col_one_ref, col_two_ref,
+    strip, boxes, boxes_in, freq, freq_mid, freq_ready, freq_in, held, to_z, landed, sums, got, local, load_sem, send, recv,
 ):
     rows, y, z, q, p = place()
     before, after = lax.rem(z + NZ - 1, NZ), lax.rem(z + 1, NZ)
     barrier = pltpu.get_barrier_semaphore()
-    load_one = pltpu.make_async_copy(one_hbm, one_ref, local.at[0])
-    load_two = pltpu.make_async_copy(two_hbm, two_ref, local.at[1])
-    load_one.start()
-    load_two.start()
-
-    def greet_z(k):
+    loads = []
+    for index, (source, target) in enumerate(
+        (
+            (row_one_hbm, row_one_ref),
+            (row_two_hbm, row_two_ref),
+            (box_one_hbm, box_one_ref),
+            (col_one_hbm, col_one_ref),
+            (col_two_hbm, col_two_ref),
+        )
+    ):
+        loads.append(pltpu.make_async_copy(source, target, load_sem.at[index]))
+        loads[-1].start()
+
+    for k in far_first(NZ):
         signal(barrier, lax.rem(z + k, NZ) * NQ + q, y)
-
-    def greet_after(k):
-        signal(barrier, after * NQ + k // NY, lax.rem(k, NY))
-
-    loop(NZ, greet_z, 1)
+    loop(32, lambda k: signal(barrier, after * NQ + k // NY, lax.rem(k, NY)))
     signal_plane(barrier, z, p)
-    loop(32, greet_after)
 
     lane = lax.broadcasted_iota(jnp.int32, (32, 256), 1)
 
@@ -197,20 +207,20 @@
         entry = jnp.where(near >= 0, near * NY + y, 32 + near + NQ)
         home = lax.rem(rows - d + NBAND, NBAND)
         for s in range(4):
-            left = (code_ref[home // NQ, lax.rem(home, NQ) * 16 + y * 4 + s] >> 12) & 4095
+            left = tops_ref[(y * 4 + s) * 2 + 1, home] & 4095
             block = left >> 8
             offset = left & 255
             first = band_ref[block].astype(f32)
             second = band_ref[jnp.minimum(block + 1, 15)].astype(f32)
             picked = jnp.where(lane >= offset, first, second)
-            shift = (table_ref[entry, 0, 2 * s + 1] - offset) & 255
+            shift = (table_ref[entry, 1, s] - offset) & 255
             strip[pl.ds(32 * s, 32), :] = pltpu.roll(picked, shift, 1)
         boxes[:, d] = strip[...].T.reshape(32, 8, 128).astype(bf16)
 
     loop(REACH, one_band)
     pl.semaphore_wait(barrier, 15 + 63)
 
-    here = p
+    here = p * REACH
     for level in range(NQ):
 
         @pl.when(q == level)
@@ -218,83 +228,66 @@
             near, far = level + 1, REACH - 1 - level
 
             def send_far(k):
+                other = lax.rem(p + 16 + k, 32)
                 remote(
-                    boxes.at[k, pl.ds(near, far)], boxes_out.at[pl.ds(here * REACH + near, far)],
-                    send.at[2], recv.at[2], before * NQ + k // NY, lax.rem(k, NY),
+                    boxes.at[other, pl.ds(near, far)], boxes_in.at[pl.ds(here + near, far)],
+                    send.at[2], recv.at[2], before * NQ + other // NY, lax.rem(other, NY),
                 ).start()
 
             def send_near(k):
                 other = lax.rem(p + k, 32)
                 remote(
-                    boxes.at[other, pl.ds(0, near)], boxes_out.at[pl.ds(here * REACH, near)],
+                    boxes.at[other, pl.ds(0, near)], boxes_in.at[pl.ds(here, near)],
                     send.at[1], recv.at[1], z * NQ + other // NY, lax.rem(other, NY),
                 ).start()
 
             loop(32, send_far)
             loop(32, send_near, 1)
-            pltpu.make_async_copy(boxes.at[here, pl.ds(0, near)], boxes_out.at[pl.ds(here * REACH, near)], local.at[2]).start()
-
-    load_one.wait()
-    load_two.wait()
+            pltpu.make_async_copy(boxes.at[p, pl.ds(0, near)], boxes_in.at[pl.ds(here, near)], local.at[0]).start()
+
+    loads[0].wait()
+    loads[1].wait()
     real, imag = [], []
-    cos_all, sin_all = twist_ref[y, 0], twist_ref[y, 1]
+    cos_all, sin_all = row_twist_ref[y, 0], row_twist_ref[y, 1]
     for side in range(2):
         pixels = band_ref[:, :].reshape(8, 2, 32, 256)[:, side].reshape(256, 256)
-        section = exact_product(one_ref, pixels, mm)
+        section = exact_product(row_one_ref, pixels, mm)
         cos = jnp.broadcast_to(cos_all[:, 256 * side : 256 * side + 256][:, None, :], (8, 32, 256)).reshape(256, 256)
         sin = jnp.broadcast_to(sin_all[:, 256 * side : 256 * side + 256][:, None, :], (8, 32, 256)).reshape(256, 256)
         real.append(section[:256] * cos + section[256:] * sin)
         imag.append(section[256:] * cos - section[:256] * sin)
     turned = jnp.concatenate(real + imag, axis=1)
-    result = full_product(two_ref, turned, mmt).astype(bf16)
+    result = full_product(row_two_ref, turned, mmt).astype(bf16)
     freq[0] = result[:, :128]
     freq[1] = result[:, 128:]
 
-    def send_z(k):
+    for k in far_first(NQ):
+        other = lax.rem(q + k, NQ)
+        remote(freq.at[:, pl.ds(32 * other, 32)], freq_mid.at[:, q], send.at[3], recv.at[3], z * NQ + other, y).start()
+    own_mid = pltpu.make_async_copy(freq.at[:, pl.ds(32 * q, 32)], freq_mid.at[:, q], local.at[1])
+    own_mid.start()
+    own_mid.wait()
+    wait_for(freq_mid.at[:, pl.ds(0, NQ - 1)], send.at[3])
+    wait_for(freq_mid.at[:, pl.ds(0, NQ - 1)], recv.at[3])
+    for h in range(2):
+        freq_ready[h] = freq_mid[h].reshape(NQ, NZ, 2, 128)
+    for k in far_first(NZ):
         other = lax.rem(z + k, NZ)
-        remote(
-            freq.at[:, pl.ds(16 * other, 16)], freq_out.at[:, z], send.at[0], recv.at[0], other * NQ + q, y
-        ).start()
-
-    loop(NZ, send_z, 1)
-    own = pltpu.make_async_copy(freq.at[:, pl.ds(16 * z, 16)], freq_out.at[:, z], local.at[3])
-    own.start()
+        remote(freq_ready.at[:, :, other], freq_in.at[:, :, z], send.at[4], recv.at[4], other * NQ + q, y).start()
+    own_freq = pltpu.make_async_copy(freq_ready.at[:, :, z], freq_in.at[:, :, z], local.at[1])
+    own_freq.start()
 
     for level in range(NQ):
 
         @pl.when(q == level)
         def _():
             near, far = level + 1, REACH - 1 - level
-            wait_for(boxes.at[0, pl.ds(0, near)], local.at[2])
+            wait_for(boxes.at[0, pl.ds(0, near)], local.at[0])
             wait_for(boxes.at[pl.ds(0, 32), pl.ds(0, far)], send.at[2])
             wait_for(boxes.at[pl.ds(0, 31), pl.ds(0, near)], send.at[1])
-            wait_for(whole_pieces(boxes_out, 144 - near), recv.at[1])
-
-    wait_for(whole_pieces(boxes_out, 144), recv.at[2])
-    own.wait()
-    wait_for(freq_out.at[:, pl.ds(0, 15)], send.at[0])
-    wait_for(freq_out.at[:, pl.ds(0, 15)], recv.at[0])
-
-
-def sum_kernel(
-    code_ref, table_ref, labels_ref, boxes_ref, freq_ref, one_hbm, two_ref, twist_ref, quarter_ref, col_one_hbm, col_twist_ref,
-    col_two_hbm, power_ref, means_ref, one_ref, col_one_ref, col_two_ref, held, to_z, landed, sums, got, freq, local, send, recv,
-):
-    rows, y, z, q, p = place()
-    barrier = pltpu.get_barrier_semaphore()
-    loads = [
-        pltpu.make_async_copy(one_hbm, one_ref, local.at[4]),
-        pltpu.make_async_copy(col_one_hbm, col_one_ref, local.at[5]),
-        pltpu.make_async_copy(col_two_hbm, col_two_ref, local.at[6]),
-    ]
-    for load in loads:
-        load.start()
-
-    def greet_z(k):
-        signal(barrier, lax.rem(z + k, NZ) * NQ + q, y)
-
-    loop(NZ, greet_z, 1)
-    signal_plane(barrier, z, p)
+            wait_for(boxes_in.at[pl.ds(0, 144 - near)], recv.at[1])
+
+    wait_for(boxes_in.at[pl.ds(0, 144)], recv.at[2])
 
     lane = lax.broadcasted_iota(jnp.int32, (8, 128), 1)
     group = lane >> 5
@@ -304,7 +297,7 @@
         j = home & 3
         spun = []
         for d in range(REACH):
-            piece = boxes_ref[(((q0 + d) & 7) * NY + j) * REACH + d].astype(f32)
+            piece = boxes_in[(((q0 + d) & 7) * NY + j) * REACH + d].astype(f32)
             spun.append([piece] + [pltpu.roll(piece, 32 * turns, 1) for turns in range(1, 4)])
 
         def joined(first, s):
@@ -315,60 +308,53 @@
 
         for s in range(4):
             slot = home * 4 + s
-            top = ((code_ref[z, slot] & 4095) - rows_of(z, q0)) & 255
-            shift = (table_ref[home, 0, 2 * s] - top) & 255
+            band = z * NQ + q0
+            top = (tops_ref[(j * 4 + s) * 2, band] - band * 32) & 255
+            shift = (table_ref[home, 0, s] - top) & 255
             low = jnp.where(lane >= top, joined(0, s), spun[8][(0 - s) % 4])
             held[slot] = pltpu.roll(jnp.concatenate([low, joined(4, s)], axis=1), shift, 1)
 
     loop(32, one_home)
 
-    kinds = lax.broadcasted_iota(jnp.int32, (64, 128), 0)
-    chosen = (kinds == (labels_ref[pl.ds(z, 1), :] >> 24)).astype(bf16)
+    labels = jnp.where(live_ref[...] == 1, class_ref[...], CLASSES)
+    plane_labels = pltpu.roll(labels, lax.rem(NBAND - z * NQ, NBAND), 1)
+    kind_lane = lax.broadcasted_iota(jnp.int32, (16, 128), 1)
+    chosen = jnp.concatenate([(plane_labels[:, k : k + 1] == kind_lane).astype(f32) for k in range(NQ)], axis=0)
+    chosen = chosen.T[:64].astype(bf16)
     columns = [mm(chosen, held[:, c, :].astype(bf16)) for c in range(8)]
-    loads[0].wait()
-    main = full_product(one_ref, jnp.concatenate([column[:48] for column in columns], axis=0), mmt)
-    rest = full_product(one_ref, jnp.concatenate([column[48:50] for column in columns], axis=0), mmt)
+    loads[2].wait()
+    main = full_product(box_one_ref, jnp.concatenate([column[:48] for column in columns], axis=0), mmt)
+    rest = full_product(box_one_ref, jnp.concatenate([column[48:50] for column in columns], axis=0), mmt)
     rest = jnp.concatenate([rest[64 * k : 64 * k + 64] for k in range(NQ)], axis=1)
     for k in range(NQ):
         for t in range(3):
             to_z[3 * k + t] = main[64 * k : 64 * k + 64, 128 * t : 128 * t + 128].reshape(NZ, 4, 128).astype(bf16)
     to_z[24] = rest.reshape(NZ, 4, 128).astype(bf16)
-    pl.semaphore_wait(barrier, 15 + 31)
-
-    def send_z(k):
+
+    for k in far_first(NZ):
         other = lax.rem(z + k, NZ)
         remote(to_z.at[:, other], landed.at[:, z], send.at[0], recv.at[0], other * NQ + q, y).start()
-
-    def send_q(k):
-        other = lax.rem(q + k, NQ)
-        remote(freq_ref.at[:, :, other], freq.at[:, q], send.at[2], recv.at[2], z * NQ + other, y).start()
-
-    loop(NQ, send_q, 1)
-    loop(NZ, send_z, 1)
-    own = [
-        pltpu.make_async_copy(to_z.at[:, z], landed.at[:, z], local.at[0]),
-        pltpu.make_async_copy(freq_ref.at[:, :, q], freq.at[:, q], local.at[1]),
-    ]
-    for copy in own:
-        copy.start()
+    own = pltpu.make_async_copy(to_z.at[:, z], landed.at[:, z], local.at[2])
+    own.start()
 
     cos_y, sin_y = quarter_ref[y, 0][None, :], quarter_ref[y, 1][None, :]
-    cos = twist_ref[0] * cos_y - twist_ref[1] * sin_y
-    sin = twist_ref[1] * cos_y + twist_ref[0] * sin_y
-
+    cos = box_twist_ref[0] * cos_y - box_twist_ref[1] * sin_y
+    sin = box_twist_ref[1] * cos_y + box_twist_ref[0] * sin_y
+
+    kinds = lax.broadcasted_iota(jnp.int32, (64, 128), 0)
     counts = jnp.zeros((64, 128), f32)
-    for k in range(NZ):
-        counts = counts + (kinds == (labels_ref[k : k + 1, :] >> 24)).astype(f32)
+    for k in range(16):
+        counts = counts + (kinds == labels[k : k + 1, :]).astype(f32)
     inverse = 1.0 / (BOX * jnp.maximum(jnp.sum(counts, axis=1, keepdims=True), 1.0))
 
-    for load in loads[1:]:
-        load.wait()
-    own[1].wait()
-    wait_for(freq.at[:, pl.ds(0, NQ - 1)], send.at[2])
-    wait_for(freq.at[:, pl.ds(0, NQ - 1)], recv.at[2])
+    loads[3].wait()
+    loads[4].wait()
+    own_freq.wait()
+    wait_for(freq_in.at[:, :, pl.ds(0, NZ - 1)], send.at[4])
+    wait_for(freq_in.at[:, :, pl.ds(0, NZ - 1)], recv.at[4])
     col_cos, col_sin = col_twist_ref[0], col_twist_ref[1]
     for h in range(2):
-        section = exact_product(col_one_ref, freq[h].reshape(256, 128), mm)
+        section = exact_product(col_one_ref, freq_in[h].reshape(256, 128), mm)
         real = section[:128] * col_cos + section[128:] * col_sin
         imag = section[128:] * col_cos - section[:128] * col_sin
         result = full_product(col_two_ref, jnp.concatenate([real, imag], axis=1), mmt)
@@ -376,7 +362,7 @@
         for tau in range(32):
             power_ref[0, 4 * h : 4 * h + 4, 128 * tau : 128 * tau + 128] = power[4 * tau : 4 * tau + 4]
 
-    own[0].wait()
+    own.wait()
     wait_for(landed.at[:, pl.ds(0, 15)], send.at[0])
     wait_for(landed.at[:, pl.ds(0, 15)], recv.at[0])
     last = jnp.sum(landed[24].astype(f32), axis=0)
@@ -388,20 +374,20 @@
     def send_plane(k):
         other = lax.rem(p + k, 32)
         there = other // NY
-        remote(sums.at[there], got.at[p], send.at[1], recv.at[1], z * NQ + there, lax.rem(other, NY)).start()
+        remote(sums.at[there], got.at[p], send.at[5], recv.at[5], z * NQ + there, lax.rem(other, NY)).start()
 
     loop(32, send_plane, 1)
-    mine = pltpu.make_async_copy(sums.at[q], got.at[p], local.at[2])
+    mine = pltpu.make_async_copy(sums.at[q], got.at[p], local.at[3])
     mine.start()
     mine.wait()
-    wait_for(got.at[pl.ds(0, 31)], send.at[1])
-    wait_for(got.at[pl.ds(0, 31)], recv.at[1])
+    wait_for(got.at[pl.ds(0, 31)], send.at[5])
+    wait_for(got.at[pl.ds(0, 31)], recv.at[5])
 
     pieces = []
     for a in range(2):
         for t in range(4):
             pieces.append(jnp.concatenate([got[:, t, a, :], got[:, t, 2 + a, :]], axis=0))
-    section = full_product(two_ref, jnp.concatenate(pieces, axis=1), mm)
+    section = full_product(box_two_ref, jnp.concatenate(pieces, axis=1), mm)
     lanes = lax.broadcasted_iota(jnp.int32, (48, 384), 1)
     pick = (lax.rem(lanes, 48) == lax.broadcasted_iota(jnp.int32, (48, 384), 0)).astype(bf16)
     lanes = lax.broadcasted_iota(jnp.int32, (16, 128), 1)
@@ -417,14 +403,6 @@
             means_ref[48:50, part, a, :] = total[:2] * inverse[48:50]
 
 
-def rows_of(z, q0):
-    return (z * NQ + q0) * 32
-
-
-def whole_pieces(ref, count):
-    return ref.at[pl.ds(0, count)]
-
-
 def call(kernel, outs, ins, out_specs, scratch=(), collective=None, name=None):
     params = dict(has_side_effects=True, collective_id=collective) if collective is not None else {}
     return pl.pallas_call(
@@ -448,13 +426,14 @@
 
 def per_device(micrograph, box_tops, box_live, box_class, box_shift):
     consts = {name: jnp.asarray(value) for name, value in tables().items()}
-    labels = jnp.where(box_live == 1, box_class, CLASSES)
-    codes = ((labels * 4096 + box_tops[..., 1]) * 4096 + box_tops[..., 0]).reshape(NZ, 128)
-
-    shifts = jnp.pad(box_shift.reshape(1, 8), ((0, 0), (0, 120)))
+    tops = box_tops.transpose(1, 2, 3, 0).reshape(32, NBAND)
+    classes = box_class.transpose(1, 2, 0).reshape(16, NBAND)
+    live = box_live.transpose(1, 2, 0).reshape(16, NBAND)
+    shifts = box_shift.transpose(0, 1, 3, 2).reshape(2, 4)
+
     band, table = call(
         gather_kernel,
-        (shape(16, 32, 256), shape(32 + NQ, 1, 128, dtype=jnp.int32)),
+        (shape(16, 32, 256), shape(32 + NQ, 2, 4, dtype=jnp.int32)),
         [ANY, VMEM],
         (VMEM, VMEM),
         (sems(5), sems(2), sems(2)),
@@ -462,51 +441,40 @@
         name="gather",
     )(micrograph, shifts)
 
-    freq, boxes = call(
-        spread_kernel,
-        (shape(2, NZ, 16, 128), shape(32 * REACH, 8, 128)),
-        [SMEM, SMEM, VMEM, VMEM, ANY, ANY],
+    return call(
+        main_kernel,
+        (shape(1, 8, NPIX, dtype=f32), shape(CLASSES, 2, 2, 64, dtype=f32)),
+        [SMEM, SMEM] + [VMEM] * 8 + [ANY] * 5,
         (VMEM, VMEM),
         (
             pltpu.VMEM((2, 512, 256), bf16),
             pltpu.VMEM((2, 256, 1024), bf16),
-            pltpu.VMEM((128, 256), f32),
-            pltpu.VMEM((32, REACH, 8, 128), bf16),
-            pltpu.VMEM((2, 256, 128), bf16),
-            sems(4),
-            sems(3),
-            sems(3),
-        ),
-        collective=1,
-        name="spread",
-    )(codes, table, band, consts["row_twist"], consts["row_one"], consts["row_two"])
-
-    power, means = call(
-        sum_kernel,
-        (shape(1, 8, NPIX, dtype=f32), shape(CLASSES, 2, 2, 64, dtype=f32)),
-        [SMEM, SMEM, VMEM, VMEM, VMEM, ANY, VMEM, VMEM, VMEM, ANY, VMEM, ANY],
-        (VMEM, VMEM),
-        (
             pltpu.VMEM((2, 512, 256), bf16),
             pltpu.VMEM((2, 256, 256), bf16),
             pltpu.VMEM((2, 256, 256), bf16),
+            pltpu.VMEM((128, 256), f32),
+            pltpu.VMEM((32, REACH, 8, 128), bf16),
+            pltpu.VMEM((32 * REACH, 8, 128), bf16),
+            pltpu.VMEM((2, 256, 128), bf16),
+            pltpu.VMEM((2, NQ, 32, 128), bf16),
+            pltpu.VMEM((2, NQ, NZ, 2, 128), bf16),
+            pltpu.VMEM((2, NQ, NZ, 2, 128), bf16),
             pltpu.VMEM((128, 8, 256), f32),
             pltpu.VMEM((25, NZ, 4, 128), bf16),
             pltpu.VMEM((25, NZ, 4, 128), bf16),
             pltpu.VMEM((NQ, 4, 4, 128), f32),
             pltpu.VMEM((32, 4, 4, 128), f32),
-            pltpu.VMEM((2, NQ, NZ, 2, 128), bf16),
-            sems(7),
-            sems(3),
-            sems(3),
+            sems(4),
+            sems(5),
+            sems(6),
+            sems(6),
         ),
-        collective=2,
-        name="sums",
+        collective=1,
+        name="main",
     )(
-        codes, table, codes, boxes, freq.reshape(2, NZ, NQ, 2, 128), consts["box_one"], consts["box_two"], consts["box_twist"],
-        consts["box_quarter"], consts["col_one"], consts["col_twist"], consts["col_two"],
+        tops, table, classes, live, band, consts["row_twist"], consts["box_twist"], consts["box_quarter"], consts["col_twist"],
+        consts["box_two"], consts["row_one"], consts["row_two"], consts["box_one"], consts["col_one"], consts["col_two"],
     )
-    return power, means
 
 
 def solution(mesh):

time: 91.8 us -> 83.2 us (0.906)
  Pallas kernels: 85.3 us -> 80 us
  local copies, waits for them, and re-layouts: 5.47 us -> 2.25 us
    pallas_call x3 -> x2, Pallas kernels: 85.3 us -> 80 us  [the longest x1 59.2 us: per_device(): call(main_kernel, (shape(1, 8, NPIX, dtype=f32), shape(CLASSES, 2, 2, 64,...]
    reshape x2 -> x0, local copies, waits for them, and re-layouts: 0.95 us -> none  [the longest x1 0.86 us: per_device(): ((labels * 4096 + box_tops[..., 1]) * 4096 + box_tops[..., 0]).reshape(NZ...]
    unnamed x9 -> x4, local copies, waits for them, and re-layouts: 3.02 us -> 2.25 us
where the time goes in v3:
time: 83.2 us; the launch traced here: 82.9 us
  Pallas kernels  80 us (96%)
  local copies, waits for them, and re-layouts  2.25 us (3%)
    pallas_call x1, Pallas kernels, per_device(): call(main_kernel, (shape(1, 8, NPIX, dtype=f32), shape(CLASSES, 2, 2, 64,...  59.2 us
    pallas_call x1, Pallas kernels, per_device(): call(gather_kernel, (shape(16, 32, 256), shape(32 + NQ, 2, 4, dtype=jnp.i...  20.8 us
    unnamed x4, local copies, waits for them, and re-layouts  2.25 us

profile of v3, /device:TPU:1, one launch (start us, length us, event | category | flops | bytes accessed | tf_op | source)
XLA Modules:
  0.0 82.9 jit_solution(9109420246349790956)
XLA Ops:
  0.6 20.8 %gather.1 = (bf16[16,32,256]{2,1,0:T(8,128)(2,1)}, s32[40,2,4]{2,1,0:T(2,128)}) custom-call(bf16[32,1024]{1,0:T(8,128)(2,1)} %mic_ref.1, s32[2,4]{1,0:T(2,128)} %bitcast.15), custom_call_target="tpu_custom_call" | custom-call | tf_op jit(solution)/shard_map/gather/pallas_call | solution.py:434
  21.5 59.2 %main.1 = (f32[1,8,4096]{2,1,0:T(8,128)}, f32[50,2,2,64]{3,2,1,0:T(2,128)}) custom-call(s32[32,128]{1,0:T(8,128)} %bitcast.12, s32[40,2,4]{2,1,0:T(2,128)} %get-tuple-element.4.table_ref, s32[16,128]{1,0:T(8,128)} %bitcast.13, s32[16,128]{1,0:T(8,128)} %bitcast.14, bf16[16,32,256]{2,1,0:T(8,128)(2,1)} %get-tuple-element.5.band_ref, ...), custom_call_target="tpu_custom_call" | custom-call | tf_op jit(solution)/shard_map/main/pallas_call | solution.py:444
  80.6 0.0 copy-start
  80.6 1.6 %copy.19 = f32[1,8,4096]{2,1,0:T(8,128)} copy(f32[1,8,4096]{2,1,0:T(8,128)} %get-tuple-element.8) | data formatting | bytes 262144
  82.3 0.0 copy-done
  82.3 0.6 copy.20
Async XLA Ops:
  80.6 1.6 %copy-start = (f32[50,2,2,64]{3,2,1,0:T(2,128)S(1)}, f32[50,2,2,64]{3,2,1,0:T(2,128)}, u32[]{:S(2)}) copy-start(f32[50,2,2,64]{3,2,1,0:T(2,128)} %get-tuple-element.9) | copy-start | bytes 153604

commit v4 on v3

--- a/solution.py
+++ b/solution.py
@@ -117,12 +117,12 @@
     pltpu.make_async_copy(ref, ref, sem).wait()
 
 
-def loop(count, body, start=0):
+def loop(count, body, start=0, unroll=1):
     def step(index, carry):
         body(index)
         return carry
 
-    lax.fori_loop(start, count, step, 0)
+    lax.fori_loop(start, count, step, 0, unroll=unroll)
 
 
 def signal_plane(barrier, z, p):
@@ -133,55 +133,30 @@
     loop(32, greet, 1)
 
 
-def gather_kernel(mic_ref, shift_ref, band_ref, table_ref, local, send, recv):
-    rows, y, z, q, p = place()
-    before, after = lax.rem(z + NZ - 1, NZ), lax.rem(z + 1, NZ)
-    own = []
-    for a in range(4):
-        own.append(pltpu.make_async_copy(mic_ref.at[:, pl.ds(256 * a, 256)], band_ref.at[NY * y + a], local.at[a]))
-    own.append(pltpu.make_async_copy(shift_ref, table_ref.at[p], local.at[4]))
-    for copy in own:
-        copy.start()
-    barrier = pltpu.get_barrier_semaphore()
-    signal_plane(barrier, z, p)
-    for k in range(NQ):
-        signal(barrier, before * NQ + k, y)
-    for copy in own:
-        copy.wait()
-    pl.semaphore_wait(barrier, 31 + NQ)
-
-    mine = band_ref.at[pl.ds(NY * y, 4)]
-    for k in range(1, NY):
-        remote(mine, mine, send.at[0], recv.at[0], rows, lax.rem(y + k, NY)).start()
-    for k in range(NQ):
-        remote(table_ref.at[p], table_ref.at[32 + q], send.at[1], recv.at[1], after * NQ + k, y).start()
-
-    def tell(k):
-        other = lax.rem(p + k, 32)
-        remote(
-            table_ref.at[p], table_ref.at[p], send.at[1], recv.at[1], z * NQ + other // NY, lax.rem(other, NY)
-        ).start()
-
-    loop(32, tell, 1)
-    wait_for(band_ref.at[pl.ds(0, 12)], send.at[0])
-    wait_for(table_ref.at[pl.ds(0, 31 + NQ)], send.at[1])
-    wait_for(band_ref.at[pl.ds(0, 12)], recv.at[0])
-    wait_for(table_ref.at[pl.ds(0, 31 + NQ)], recv.at[1])
-
-
 def far_first(count):
     return sorted(range(1, count), key=lambda k: -min(k, count - k))
 
 
 def main_kernel(
-    tops_ref, table_ref, class_ref, live_ref, band_ref, row_twist_ref, box_twist_ref, quarter_ref, col_twist_ref, box_two_ref,
+    tops_ref, shift_ref, class_ref, live_ref, mic_ref, row_twist_ref, box_twist_ref, quarter_ref, col_twist_ref, box_two_ref,
     row_one_hbm, row_two_hbm, box_one_hbm, col_one_hbm, col_two_hbm, power_ref, means_ref,
-    row_one_ref, row_two_ref, box_one_ref, col_one_ref, col_two_ref,
-    strip, boxes, boxes_in, freq, freq_mid, freq_ready, freq_in, held, to_z, landed, sums, got, local, load_sem, send, recv,
+    row_one_ref, row_two_ref, box_one_ref, col_one_ref, col_two_ref, band_ref, table_in, table_ref,
+    boxes, boxes_in, freq, freq_mid, freq_ready, freq_in, held, to_z, landed, sums, got, local, load_sem, send, recv,
 ):
     rows, y, z, q, p = place()
     before, after = lax.rem(z + NZ - 1, NZ), lax.rem(z + 1, NZ)
     barrier = pltpu.get_barrier_semaphore()
+    for k in far_first(NZ):
+        signal(barrier, lax.rem(z + k, NZ) * NQ + q, y)
+    loop(32, lambda k: signal(barrier, after * NQ + k // NY, lax.rem(k, NY)))
+    loop(NQ, lambda k: signal(barrier, before * NQ + k, y))
+    signal_plane(barrier, z, p)
+
+    own = [pltpu.make_async_copy(shift_ref, table_in.at[p], local.at[4])]
+    for a in range(4):
+        own.append(pltpu.make_async_copy(mic_ref.at[:, pl.ds(256 * a, 256)], band_ref.at[NY * y + a], local.at[a]))
+    for copy in own:
+        copy.start()
     loads = []
     for index, (source, target) in enumerate(
         (
@@ -194,11 +169,28 @@
     ):
         loads.append(pltpu.make_async_copy(source, target, load_sem.at[index]))
         loads[-1].start()
-
-    for k in far_first(NZ):
-        signal(barrier, lax.rem(z + k, NZ) * NQ + q, y)
-    loop(32, lambda k: signal(barrier, after * NQ + k // NY, lax.rem(k, NY)))
-    signal_plane(barrier, z, p)
+    for copy in own:
+        copy.wait()
+    pl.semaphore_wait(barrier, 15 + 63 + NQ)
+
+    mine = band_ref.at[pl.ds(NY * y, 4)]
+    for k in (2, 1, 3):
+        remote(mine, mine, send.at[6], recv.at[6], rows, lax.rem(y + k, NY)).start()
+    for k in range(NQ):
+        remote(table_in.at[p], table_in.at[32 + q], send.at[7], recv.at[7], after * NQ + k, y).start()
+
+    def tell(k):
+        other = lax.rem(p + k, 32)
+        remote(
+            table_in.at[p], table_in.at[p], send.at[7], recv.at[7], z * NQ + other // NY, lax.rem(other, NY)
+        ).start()
+
+    loop(32, tell, 1)
+    wait_for(table_in.at[pl.ds(0, 31 + NQ)], recv.at[7])
+    to_scalar = pltpu.make_async_copy(table_in, table_ref, local.at[0])
+    to_scalar.start()
+    wait_for(band_ref.at[pl.ds(0, 12)], recv.at[6])
+    to_scalar.wait()
 
     lane = lax.broadcasted_iota(jnp.int32, (32, 256), 1)
 
@@ -206,6 +198,7 @@
         near = q - d
         entry = jnp.where(near >= 0, near * NY + y, 32 + near + NQ)
         home = lax.rem(rows - d + NBAND, NBAND)
+        strips = []
         for s in range(4):
             left = tops_ref[(y * 4 + s) * 2 + 1, home] & 4095
             block = left >> 8
@@ -214,11 +207,10 @@
             second = band_ref[jnp.minimum(block + 1, 15)].astype(f32)
             picked = jnp.where(lane >= offset, first, second)
             shift = (table_ref[entry, 1, s] - offset) & 255
-            strip[pl.ds(32 * s, 32), :] = pltpu.roll(picked, shift, 1)
-        boxes[:, d] = strip[...].T.reshape(32, 8, 128).astype(bf16)
-
-    loop(REACH, one_band)
-    pl.semaphore_wait(barrier, 15 + 63)
+            strips.append(pltpu.roll(picked, shift, 1))
+        boxes[:, d] = jnp.concatenate(strips, axis=0).T.reshape(32, 8, 128).astype(bf16)
+
+    loop(REACH, one_band, unroll=3)
 
     here = p * REACH
     for level in range(NQ):
@@ -226,24 +218,35 @@
         @pl.when(q == level)
         def _():
             near, far = level + 1, REACH - 1 - level
-
-            def send_far(k):
-                other = lax.rem(p + 16 + k, 32)
-                remote(
-                    boxes.at[other, pl.ds(near, far)], boxes_in.at[pl.ds(here + near, far)],
-                    send.at[2], recv.at[2], before * NQ + other // NY, lax.rem(other, NY),
-                ).start()
-
-            def send_near(k):
-                other = lax.rem(p + k, 32)
-                remote(
-                    boxes.at[other, pl.ds(0, near)], boxes_in.at[pl.ds(here, near)],
-                    send.at[1], recv.at[1], z * NQ + other // NY, lax.rem(other, NY),
-                ).start()
-
-            loop(32, send_far)
-            loop(32, send_near, 1)
             pltpu.make_async_copy(boxes.at[p, pl.ds(0, near)], boxes_in.at[pl.ds(here, near)], local.at[0]).start()
+            for e in (0, 1, 3, 2):
+                side = lax.rem(y + e, NY)
+                group = (NY - e) % NY
+
+                def send_both(k):
+                    there = lax.rem(q + k, NQ)
+                    target = there * NY + side
+                    remote(
+                        boxes.at[target, pl.ds(near, far)], boxes_in.at[pl.ds(here + near, far)],
+                        send.at[2], recv.at[12 + group], before * NQ + there, side,
+                    ).start()
+                    remote(
+                        boxes.at[target, pl.ds(0, near)], boxes_in.at[pl.ds(here, near)],
+                        send.at[1], recv.at[8 + group], z * NQ + there, side,
+                    ).start()
+
+                def send_far_only(k):
+                    there = lax.rem(q + k, NQ)
+                    remote(
+                        boxes.at[there * NY + side, pl.ds(near, far)], boxes_in.at[pl.ds(here + near, far)],
+                        send.at[2], recv.at[12 + group], before * NQ + there, side,
+                    ).start()
+
+                loop(NQ, send_both, 1)
+                if e == 0:
+                    send_far_only(0)
+                else:
+                    send_both(0)
 
     loads[0].wait()
     loads[1].wait()
@@ -277,24 +280,11 @@
     own_freq = pltpu.make_async_copy(freq_ready.at[:, :, z], freq_in.at[:, :, z], local.at[1])
     own_freq.start()
 
-    for level in range(NQ):
-
-        @pl.when(q == level)
-        def _():
-            near, far = level + 1, REACH - 1 - level
-            wait_for(boxes.at[0, pl.ds(0, near)], local.at[0])
-            wait_for(boxes.at[pl.ds(0, 32), pl.ds(0, far)], send.at[2])
-            wait_for(boxes.at[pl.ds(0, 31), pl.ds(0, near)], send.at[1])
-            wait_for(boxes_in.at[pl.ds(0, 144 - near)], recv.at[1])
-
-    wait_for(boxes_in.at[pl.ds(0, 144)], recv.at[2])
-
     lane = lax.broadcasted_iota(jnp.int32, (8, 128), 1)
     group = lane >> 5
 
-    def one_home(home):
-        q0 = home >> 2
-        j = home & 3
+    def one_home(q0, j):
+        home = q0 * NY + j
         spun = []
         for d in range(REACH):
             piece = boxes_in[(((q0 + d) & 7) * NY + j) * REACH + d].astype(f32)
@@ -314,7 +304,20 @@
             low = jnp.where(lane >= top, joined(0, s), spun[8][(0 - s) % 4])
             held[slot] = pltpu.roll(jnp.concatenate([low, joined(4, s)], axis=1), shift, 1)
 
-    loop(32, one_home)
+    for g in (0, 1, 3, 2):
+        if g == 0:
+            for level in range(NQ):
+
+                @pl.when(q == level)
+                def _():
+                    wait_for(boxes_in.at[pl.ds(0, 36 - (level + 1))], recv.at[8])
+                    wait_for(boxes_in.at[pl.ds(0, level + 1)], local.at[0])
+
+        else:
+            wait_for(boxes_in.at[pl.ds(0, 36)], recv.at[8 + g])
+        wait_for(boxes_in.at[pl.ds(0, 36)], recv.at[12 + g])
+        j = lax.rem(y + g, NY)
+        loop(NQ, lambda q0: one_home(q0, j), unroll=4)
 
     labels = jnp.where(live_ref[...] == 1, class_ref[...], CLASSES)
     plane_labels = pltpu.roll(labels, lax.rem(NBAND - z * NQ, NBAND), 1)
@@ -371,15 +374,22 @@
             sums[k, t] = jnp.sum(landed[3 * k + t].astype(f32), axis=0)
         sums[k, 3] = last
 
-    def send_plane(k):
+    for k in far_first(32):
         other = lax.rem(p + k, 32)
         there = other // NY
         remote(sums.at[there], got.at[p], send.at[5], recv.at[5], z * NQ + there, lax.rem(other, NY)).start()
-
-    loop(32, send_plane, 1)
     mine = pltpu.make_async_copy(sums.at[q], got.at[p], local.at[3])
     mine.start()
     mine.wait()
+    for level in range(NQ):
+
+        @pl.when(q == level)
+        def _():
+            wait_for(boxes.at[pl.ds(0, 32), pl.ds(0, REACH - 1 - level)], send.at[2])
+            wait_for(boxes.at[pl.ds(0, 31), pl.ds(0, level + 1)], send.at[1])
+
+    wait_for(band_ref.at[pl.ds(0, 12)], send.at[6])
+    wait_for(table_in.at[pl.ds(0, 31 + NQ)], send.at[7])
     wait_for(got.at[pl.ds(0, 31)], send.at[5])
     wait_for(got.at[pl.ds(0, 31)], recv.at[5])
 
@@ -431,20 +441,10 @@
     live = box_live.transpose(1, 2, 0).reshape(16, NBAND)
     shifts = box_shift.transpose(0, 1, 3, 2).reshape(2, 4)
 
-    band, table = call(
-        gather_kernel,
-        (shape(16, 32, 256), shape(32 + NQ, 2, 4, dtype=jnp.int32)),
-        [ANY, VMEM],
-        (VMEM, VMEM),
-        (sems(5), sems(2), sems(2)),
-        collective=0,
-        name="gather",
-    )(micrograph, shifts)
-
     return call(
         main_kernel,
         (shape(1, 8, NPIX, dtype=f32), shape(CLASSES, 2, 2, 64, dtype=f32)),
-        [SMEM, SMEM] + [VMEM] * 8 + [ANY] * 5,
+        [SMEM, VMEM, VMEM, VMEM, ANY] + [VMEM] * 5 + [ANY] * 5,
         (VMEM, VMEM),
         (
             pltpu.VMEM((2, 512, 256), bf16),
@@ -452,7 +452,9 @@
             pltpu.VMEM((2, 512, 256), bf16),
             pltpu.VMEM((2, 256, 256), bf16),
             pltpu.VMEM((2, 256, 256), bf16),
-            pltpu.VMEM((128, 256), f32),
+            pltpu.VMEM((16, 32, 256), bf16),
+            pltpu.VMEM((32 + NQ, 2, 4), jnp.int32),
+            pltpu.SMEM((32 + NQ, 2, 4), jnp.int32),
             pltpu.VMEM((32, REACH, 8, 128), bf16),
             pltpu.VMEM((32 * REACH, 8, 128), bf16),
             pltpu.VMEM((2, 256, 128), bf16),
@@ -464,15 +466,15 @@
             pltpu.VMEM((25, NZ, 4, 128), bf16),
             pltpu.VMEM((NQ, 4, 4, 128), f32),
             pltpu.VMEM((32, 4, 4, 128), f32),
-            sems(4),
             sems(5),
-            sems(6),
-            sems(6),
+            sems(5),
+            sems(8),
+            sems(16),
         ),
-        collective=1,
+        collective=0,
         name="main",
     )(
-        tops, table, classes, live, band, consts["row_twist"], consts["box_twist"], consts["box_quarter"], consts["col_twist"],
+        tops, shifts, classes, live, micrograph, consts["row_twist"], consts["box_twist"], consts["box_quarter"], consts["col_twist"],
         consts["box_two"], consts["row_one"], consts["row_two"], consts["box_one"], consts["col_one"], consts["col_two"],
     )
 

time: 83.2 us -> 73.6 us (0.88)
  Pallas kernels: 80 us -> 70.5 us
    pallas_call x1 -> x0, Pallas kernels: 20.8 us -> none  [per_device(): call(gather_kernel, (shape(16, 32, 256), shape(32 + NQ, 2, 4, dtype=jnp.i...]
    pallas_call x1, Pallas kernels: 59.2 us -> 70.5 us  [per_device(): call(main_kernel, (shape(1, 8, NPIX, dtype=f32), shape(CLASSES, 2, 2, 64,...]
where the time goes in v4:
time: 73.6 us; the launch traced here: 73.4 us
  Pallas kernels  70.5 us (96%)
  local copies, waits for them, and re-layouts  2.25 us (3%)
    pallas_call x1, Pallas kernels, per_device(): call(main_kernel, (shape(1, 8, NPIX, dtype=f32), shape(CLASSES, 2, 2, 64,...  70.5 us
    unnamed x4, local copies, waits for them, and re-layouts  2.25 us

profile of v4, /device:TPU:1, one launch (start us, length us, event | category | flops | bytes accessed | tf_op | source)
XLA Modules:
  0.0 73.4 jit_solution(8221686600978319934)
XLA Ops:
  0.6 70.5 %main.1 = (f32[1,8,4096]{2,1,0:T(8,128)}, f32[50,2,2,64]{3,2,1,0:T(2,128)}) custom-call(s32[32,128]{1,0:T(8,128)} %bitcast.12, s32[2,4]{1,0:T(2,128)} %bitcast.15, s32[16,128]{1,0:T(8,128)} %bitcast.13, s32[16,128]{1,0:T(8,128)} %bitcast.14, bf16[32,1024]{1,0:T(8,128)(2,1)} %mic_ref.1, f32[4,2,8,512]{3,2,1,0:T(8,128)} %constant.21.clone.row_twist_ref, ...), custom_call_target="tpu_custom_call" | custom-call | tf_op jit(solution)/shard_map/main/pallas_call | solution.py:444
  71.1 0.0 copy-start
  71.1 1.6 %copy.19 = f32[1,8,4096]{2,1,0:T(8,128)} copy(f32[1,8,4096]{2,1,0:T(8,128)} %get-tuple-element.4) | data formatting | bytes 262144
  72.7 0.0 copy-done
  72.7 0.6 copy.20
Async XLA Ops:
  71.1 1.6 %copy-start = (f32[50,2,2,64]{3,2,1,0:T(2,128)S(1)}, f32[50,2,2,64]{3,2,1,0:T(2,128)}, u32[]{:S(2)}) copy-start(f32[50,2,2,64]{3,2,1,0:T(2,128)} %get-tuple-element.5) | copy-start | bytes 153604

commit v5 on v4

--- a/solution.py
+++ b/solution.py
@@ -141,7 +141,7 @@
     tops_ref, shift_ref, class_ref, live_ref, mic_ref, row_twist_ref, box_twist_ref, quarter_ref, col_twist_ref, box_two_ref,
     row_one_hbm, row_two_hbm, box_one_hbm, col_one_hbm, col_two_hbm, power_ref, means_ref,
     row_one_ref, row_two_ref, box_one_ref, col_one_ref, col_two_ref, band_ref, table_in, table_ref,
-    boxes, boxes_in, freq, freq_mid, freq_ready, freq_in, held, to_z, landed, sums, got, local, load_sem, send, recv,
+    boxes, boxes_in, freq, freq_mid, freq_ready, freq_in, held, to_z, landed, sums, got, early, local, load_sem, send, recv,
 ):
     rows, y, z, q, p = place()
     before, after = lax.rem(z + NZ - 1, NZ), lax.rem(z + 1, NZ)
@@ -331,12 +331,19 @@
     rest = jnp.concatenate([rest[64 * k : 64 * k + 64] for k in range(NQ)], axis=1)
     for k in range(NQ):
         for t in range(3):
-            to_z[3 * k + t] = main[64 * k : 64 * k + 64, 128 * t : 128 * t + 128].reshape(NZ, 4, 128).astype(bf16)
+            to_z[NQ * t + k] = main[64 * k : 64 * k + 64, 128 * t : 128 * t + 128].reshape(NZ, 4, 128).astype(bf16)
     to_z[24] = rest.reshape(NZ, 4, 128).astype(bf16)
 
     for k in far_first(NZ):
         other = lax.rem(z + k, NZ)
-        remote(to_z.at[:, other], landed.at[:, z], send.at[0], recv.at[0], other * NQ + q, y).start()
+        remote(
+            to_z.at[pl.ds(0, 16), other], landed.at[pl.ds(0, 16), z], send.at[0], recv.at[0], other * NQ + q, y
+        ).start()
+    for k in far_first(NZ):
+        other = lax.rem(z + k, NZ)
+        remote(
+            to_z.at[pl.ds(16, 9), other], landed.at[pl.ds(16, 9), z], send.at[8], recv.at[16], other * NQ + q, y
+        ).start()
     own = pltpu.make_async_copy(to_z.at[:, z], landed.at[:, z], local.at[2])
     own.start()
 
@@ -366,21 +373,57 @@
             power_ref[0, 4 * h : 4 * h + 4, 128 * tau : 128 * tau + 128] = power[4 * tau : 4 * tau + 4]
 
     own.wait()
-    wait_for(landed.at[:, pl.ds(0, 15)], send.at[0])
-    wait_for(landed.at[:, pl.ds(0, 15)], recv.at[0])
-    last = jnp.sum(landed[24].astype(f32), axis=0)
-    for k in range(NQ):
-        for t in range(3):
-            sums[k, t] = jnp.sum(landed[3 * k + t].astype(f32), axis=0)
-        sums[k, 3] = last
-
-    for k in far_first(32):
-        other = lax.rem(p + k, 32)
-        there = other // NY
-        remote(sums.at[there], got.at[p], send.at[5], recv.at[5], z * NQ + there, lax.rem(other, NY)).start()
-    mine = pltpu.make_async_copy(sums.at[q], got.at[p], local.at[3])
-    mine.start()
-    mine.wait()
+    mine = []
+    for part, blocks in enumerate((pl.ds(0, 16), pl.ds(16, 9))):
+        wait_for(landed.at[blocks, pl.ds(0, 15)], recv.at[16 * part])
+        for t in ((0, 1), (2,))[part]:
+            for k in range(NQ):
+                sums[k, t] = jnp.sum(landed[NQ * t + k].astype(f32), axis=0)
+        if part == 1:
+            last = jnp.sum(landed[24].astype(f32), axis=0)
+            for k in range(NQ):
+                sums[k, 3] = last
+        tiles = pl.ds(2 * part, 2)
+        for k in far_first(32):
+            other = lax.rem(p + k, 32)
+            there = other // NY
+            remote(
+                sums.at[there, tiles], got.at[p, tiles], send.at[(5, 9)[part]], recv.at[(5, 17)[part]],
+                z * NQ + there, lax.rem(other, NY),
+            ).start()
+        mine.append(pltpu.make_async_copy(sums.at[q, tiles], got.at[p, tiles], local.at[3 + part]))
+        mine[-1].start()
+
+    lanes = lax.broadcasted_iota(jnp.int32, (48, 384), 1)
+    pick = (lax.rem(lanes, 48) == lax.broadcasted_iota(jnp.int32, (48, 384), 0)).astype(bf16)
+    lanes = lax.broadcasted_iota(jnp.int32, (16, 128), 1)
+    pick_rest = (((lanes >> 4) == q) & ((lanes & 1) == lax.broadcasted_iota(jnp.int32, (16, 128), 0))).astype(bf16)
+
+    def turned_tiles(part):
+        pieces = []
+        for a in range(2):
+            for t in (2 * part, 2 * part + 1):
+                pieces.append(jnp.concatenate([got[:, t, a, :], got[:, t, 2 + a, :]], axis=0))
+        section = full_product(box_two_ref, jnp.concatenate(pieces, axis=1), mm)
+        at = slice(256 * part, 256 * part + 256)
+        for a in range(2):
+            real = jnp.concatenate([section[:32, 256 * a : 256 * a + 256]] * 2, axis=0)
+            imag = jnp.concatenate([section[32:, 256 * a : 256 * a + 256]] * 2, axis=0)
+            yield a, 0, halves(real * cos[:, at] + imag * sin[:, at])
+            yield a, 1, halves(imag * cos[:, at] - real * sin[:, at])
+
+    mine[0].wait()
+    wait_for(got.at[pl.ds(0, 31), pl.ds(0, 2)], recv.at[5])
+    for a, part, (high, low) in turned_tiles(0):
+        early[2 * a + part] = mmt(pick[:, :256], high) + mmt(pick[:, :256], low)
+    mine[1].wait()
+    wait_for(got.at[pl.ds(0, 31), pl.ds(0, 2)], recv.at[17])
+    for a, part, (high, low) in turned_tiles(1):
+        total = mmt(pick[:, 256:], high[:, :128]) + mmt(pick[:, 256:], low[:, :128])
+        means_ref[0:48, part, a, :] = (early[2 * a + part] + total) * inverse[:48]
+        total = mmt(pick_rest, high[:, 128:]) + mmt(pick_rest, low[:, 128:])
+        means_ref[48:50, part, a, :] = total[:2] * inverse[48:50]
+
     for level in range(NQ):
 
         @pl.when(q == level)
@@ -390,27 +433,10 @@
 
     wait_for(band_ref.at[pl.ds(0, 12)], send.at[6])
     wait_for(table_in.at[pl.ds(0, 31 + NQ)], send.at[7])
-    wait_for(got.at[pl.ds(0, 31)], send.at[5])
-    wait_for(got.at[pl.ds(0, 31)], recv.at[5])
-
-    pieces = []
-    for a in range(2):
-        for t in range(4):
-            pieces.append(jnp.concatenate([got[:, t, a, :], got[:, t, 2 + a, :]], axis=0))
-    section = full_product(box_two_ref, jnp.concatenate(pieces, axis=1), mm)
-    lanes = lax.broadcasted_iota(jnp.int32, (48, 384), 1)
-    pick = (lax.rem(lanes, 48) == lax.broadcasted_iota(jnp.int32, (48, 384), 0)).astype(bf16)
-    lanes = lax.broadcasted_iota(jnp.int32, (16, 128), 1)
-    pick_rest = (((lanes >> 4) == q) & ((lanes & 1) == lax.broadcasted_iota(jnp.int32, (16, 128), 0))).astype(bf16)
-    for a in range(2):
-        real = jnp.concatenate([section[:32, 512 * a : 512 * a + 512]] * 2, axis=0)
-        imag = jnp.concatenate([section[32:, 512 * a : 512 * a + 512]] * 2, axis=0)
-        for part, value in enumerate((real * cos + imag * sin, imag * cos - real * sin)):
-            high, low = halves(value)
-            total = mmt(pick, high[:, :384]) + mmt(pick, low[:, :384])
-            means_ref[0:48, part, a, :] = total * inverse[:48]
-            total = mmt(pick_rest, high[:, 384:]) + mmt(pick_rest, low[:, 384:])
-            means_ref[48:50, part, a, :] = total[:2] * inverse[48:50]
+    wait_for(landed.at[pl.ds(0, 16), pl.ds(0, 15)], send.at[0])
+    wait_for(landed.at[pl.ds(16, 9), pl.ds(0, 15)], send.at[8])
+    wait_for(got.at[pl.ds(0, 31), pl.ds(0, 2)], send.at[5])
+    wait_for(got.at[pl.ds(0, 31), pl.ds(0, 2)], send.at[9])
 
 
 def call(kernel, outs, ins, out_specs, scratch=(), collective=None, name=None):
@@ -443,7 +469,7 @@
 
     return call(
         main_kernel,
-        (shape(1, 8, NPIX, dtype=f32), shape(CLASSES, 2, 2, 64, dtype=f32)),
+        (pltpu.VMEM((1, 8, NPIX), f32), pltpu.VMEM((CLASSES, 2, 2, 64), f32)),
         [SMEM, VMEM, VMEM, VMEM, ANY] + [VMEM] * 5 + [ANY] * 5,
         (VMEM, VMEM),
         (
@@ -466,10 +492,11 @@
             pltpu.VMEM((25, NZ, 4, 128), bf16),
             pltpu.VMEM((NQ, 4, 4, 128), f32),
             pltpu.VMEM((32, 4, 4, 128), f32),
+            pltpu.VMEM((4, 48, 64), f32),
             sems(5),
             sems(5),
-            sems(8),
-            sems(16),
+            sems(10),
+            sems(18),
         ),
         collective=0,
         name="main",

time: 73.6 us -> 72.5 us (0.985)
  local copies, waits for them, and re-layouts: 2.25 us -> 1.3 us
    unnamed x4 -> x2, local copies, waits for them, and re-layouts: 2.25 us -> 1.3 us
where the time goes in v5:
time: 72.5 us; the launch traced here: 72.3 us
  Pallas kernels  70.4 us (97%)
  local copies, waits for them, and re-layouts  1.3 us (2%)
    pallas_call x1, Pallas kernels, per_device(): call(main_kernel, (pltpu.VMEM((1, 8, NPIX), f32), pltpu.VMEM((CLASSES, 2,...  70.4 us

profile of v5, /device:TPU:1, one launch (start us, length us, event | category | flops | bytes accessed | tf_op | source)
XLA Modules:
  0.0 72.3 jit_solution(14516034258372941995)
XLA Ops:
  0.6 70.4 %main.1 = (f32[1,8,4096]{2,1,0:T(8,128)S(1)}, f32[50,2,2,64]{3,2,1,0:T(2,128)S(1)}) custom-call(s32[32,128]{1,0:T(8,128)} %bitcast.12, s32[2,4]{1,0:T(2,128)} %bitcast.15, s32[16,128]{1,0:T(8,128)} %bitcast.13, s32[16,128]{1,0:T(8,128)} %bitcast.14, bf16[32,1024]{1,0:T(8,128)(2,1)} %mic_ref.1, f32[4,2,8,512]{3,2,1,0:T(8,128)} %constant.21.clone.row_twist_ref, ...), custom_call_target="tpu_custom_call" | custom-call | tf_op jit(solution)/shard_map/main/pallas_call | solution.py:470
  71.0 0.7 copy.19
  71.7 0.6 copy.20

commit v6 on v5

--- a/solution.py
+++ b/solution.py
@@ -138,9 +138,10 @@
 
 
 def main_kernel(
-    tops_ref, shift_ref, class_ref, live_ref, mic_ref, row_twist_ref, box_twist_ref, quarter_ref, col_twist_ref, box_two_ref,
+    mic_ref, shift_ref, tops_hbm, class_hbm, live_hbm, row_twist_hbm, box_twist_hbm, quarter_hbm, col_twist_hbm, box_two_hbm,
     row_one_hbm, row_two_hbm, box_one_hbm, col_one_hbm, col_two_hbm, power_ref, means_ref,
-    row_one_ref, row_two_ref, box_one_ref, col_one_ref, col_two_ref, band_ref, table_in, table_ref,
+    tops_ref, class_ref, live_ref, row_twist_ref, box_twist_ref, quarter_ref, col_twist_ref, box_two_ref,
+    row_one_ref, row_two_ref, box_one_ref, col_one_ref, col_two_ref, band_ref, table_in, table_ref, near_in, near_ref,
     boxes, boxes_in, freq, freq_mid, freq_ready, freq_in, held, to_z, landed, sums, got, early, local, load_sem, send, recv,
 ):
     rows, y, z, q, p = place()
@@ -152,7 +153,10 @@
     loop(NQ, lambda k: signal(barrier, before * NQ + k, y))
     signal_plane(barrier, z, p)
 
-    own = [pltpu.make_async_copy(shift_ref, table_in.at[p], local.at[4])]
+    own = [
+        pltpu.make_async_copy(shift_ref, table_in.at[p], local.at[4]),
+        pltpu.make_async_copy(shift_ref, near_in.at[q], local.at[5]),
+    ]
     for a in range(4):
         own.append(pltpu.make_async_copy(mic_ref.at[:, pl.ds(256 * a, 256)], band_ref.at[NY * y + a], local.at[a]))
     for copy in own:
@@ -160,11 +164,19 @@
     loads = []
     for index, (source, target) in enumerate(
         (
+            (tops_hbm, tops_ref),
+            (row_twist_hbm, row_twist_ref),
             (row_one_hbm, row_one_ref),
             (row_two_hbm, row_two_ref),
+            (class_hbm, class_ref),
+            (live_hbm, live_ref),
             (box_one_hbm, box_one_ref),
+            (quarter_hbm, quarter_ref),
+            (box_twist_hbm, box_twist_ref),
+            (col_twist_hbm, col_twist_ref),
             (col_one_hbm, col_one_ref),
             (col_two_hbm, col_two_ref),
+            (box_two_hbm, box_two_ref),
         )
     ):
         loads.append(pltpu.make_async_copy(source, target, load_sem.at[index]))
@@ -176,8 +188,12 @@
     mine = band_ref.at[pl.ds(NY * y, 4)]
     for k in (2, 1, 3):
         remote(mine, mine, send.at[6], recv.at[6], rows, lax.rem(y + k, NY)).start()
+    for k in far_first(NQ):
+        remote(
+            near_in.at[q], near_in.at[q], send.at[10], recv.at[18], z * NQ + lax.rem(q + k, NQ), y
+        ).start()
     for k in range(NQ):
-        remote(table_in.at[p], table_in.at[32 + q], send.at[7], recv.at[7], after * NQ + k, y).start()
+        remote(near_in.at[q], near_in.at[NQ + q], send.at[10], recv.at[18], after * NQ + k, y).start()
 
     def tell(k):
         other = lax.rem(p + k, 32)
@@ -186,17 +202,18 @@
         ).start()
 
     loop(32, tell, 1)
-    wait_for(table_in.at[pl.ds(0, 31 + NQ)], recv.at[7])
-    to_scalar = pltpu.make_async_copy(table_in, table_ref, local.at[0])
+    wait_for(near_in.at[pl.ds(0, 15)], recv.at[18])
+    to_scalar = pltpu.make_async_copy(near_in, near_ref, local.at[0])
     to_scalar.start()
     wait_for(band_ref.at[pl.ds(0, 12)], recv.at[6])
     to_scalar.wait()
+    loads[0].wait()
 
     lane = lax.broadcasted_iota(jnp.int32, (32, 256), 1)
 
     def one_band(d):
         near = q - d
-        entry = jnp.where(near >= 0, near * NY + y, 32 + near + NQ)
+        entry = jnp.where(near >= 0, near, 2 * NQ + near)
         home = lax.rem(rows - d + NBAND, NBAND)
         strips = []
         for s in range(4):
@@ -206,7 +223,7 @@
             first = band_ref[block].astype(f32)
             second = band_ref[jnp.minimum(block + 1, 15)].astype(f32)
             picked = jnp.where(lane >= offset, first, second)
-            shift = (table_ref[entry, 1, s] - offset) & 255
+            shift = (near_ref[entry, 1, s] - offset) & 255
             strips.append(pltpu.roll(picked, shift, 1))
         boxes[:, d] = jnp.concatenate(strips, axis=0).T.reshape(32, 8, 128).astype(bf16)
 
@@ -248,8 +265,8 @@
                 else:
                     send_both(0)
 
-    loads[0].wait()
-    loads[1].wait()
+    for load in loads[1:4]:
+        load.wait()
     real, imag = [], []
     cos_all, sin_all = row_twist_ref[y, 0], row_twist_ref[y, 1]
     for side in range(2):
@@ -280,6 +297,11 @@
     own_freq = pltpu.make_async_copy(freq_ready.at[:, :, z], freq_in.at[:, :, z], local.at[1])
     own_freq.start()
 
+    wait_for(table_in.at[pl.ds(0, 31)], recv.at[7])
+    to_scalar = pltpu.make_async_copy(table_in, table_ref, local.at[4])
+    to_scalar.start()
+    to_scalar.wait()
+
     lane = lax.broadcasted_iota(jnp.int32, (8, 128), 1)
     group = lane >> 5
 
@@ -319,13 +341,14 @@
         j = lax.rem(y + g, NY)
         loop(NQ, lambda q0: one_home(q0, j), unroll=4)
 
+    for load in loads[4:7]:
+        load.wait()
     labels = jnp.where(live_ref[...] == 1, class_ref[...], CLASSES)
     plane_labels = pltpu.roll(labels, lax.rem(NBAND - z * NQ, NBAND), 1)
     kind_lane = lax.broadcasted_iota(jnp.int32, (16, 128), 1)
     chosen = jnp.concatenate([(plane_labels[:, k : k + 1] == kind_lane).astype(f32) for k in range(NQ)], axis=0)
     chosen = chosen.T[:64].astype(bf16)
     columns = [mm(chosen, held[:, c, :].astype(bf16)) for c in range(8)]
-    loads[2].wait()
     main = full_product(box_one_ref, jnp.concatenate([column[:48] for column in columns], axis=0), mmt)
     rest = full_product(box_one_ref, jnp.concatenate([column[48:50] for column in columns], axis=0), mmt)
     rest = jnp.concatenate([rest[64 * k : 64 * k + 64] for k in range(NQ)], axis=1)
@@ -347,6 +370,8 @@
     own = pltpu.make_async_copy(to_z.at[:, z], landed.at[:, z], local.at[2])
     own.start()
 
+    for load in loads[7:]:
+        load.wait()
     cos_y, sin_y = quarter_ref[y, 0][None, :], quarter_ref[y, 1][None, :]
     cos = box_twist_ref[0] * cos_y - box_twist_ref[1] * sin_y
     sin = box_twist_ref[1] * cos_y + box_twist_ref[0] * sin_y
@@ -357,8 +382,6 @@
         counts = counts + (kinds == labels[k : k + 1, :]).astype(f32)
     inverse = 1.0 / (BOX * jnp.maximum(jnp.sum(counts, axis=1, keepdims=True), 1.0))
 
-    loads[3].wait()
-    loads[4].wait()
     own_freq.wait()
     wait_for(freq_in.at[:, :, pl.ds(0, NZ - 1)], send.at[4])
     wait_for(freq_in.at[:, :, pl.ds(0, NZ - 1)], recv.at[4])
@@ -432,7 +455,8 @@
             wait_for(boxes.at[pl.ds(0, 31), pl.ds(0, level + 1)], send.at[1])
 
     wait_for(band_ref.at[pl.ds(0, 12)], send.at[6])
-    wait_for(table_in.at[pl.ds(0, 31 + NQ)], send.at[7])
+    wait_for(table_in.at[pl.ds(0, 31)], send.at[7])
+    wait_for(near_in.at[pl.ds(0, 15)], send.at[10])
     wait_for(landed.at[pl.ds(0, 16), pl.ds(0, 15)], send.at[0])
     wait_for(landed.at[pl.ds(16, 9), pl.ds(0, 15)], send.at[8])
     wait_for(got.at[pl.ds(0, 31), pl.ds(0, 2)], send.at[5])
@@ -470,17 +494,27 @@
     return call(
         main_kernel,
         (pltpu.VMEM((1, 8, NPIX), f32), pltpu.VMEM((CLASSES, 2, 2, 64), f32)),
-        [SMEM, VMEM, VMEM, VMEM, ANY] + [VMEM] * 5 + [ANY] * 5,
+        [ANY] * 15,
         (VMEM, VMEM),
         (
+            pltpu.SMEM((32, NBAND), jnp.int32),
+            pltpu.VMEM((16, NBAND), jnp.int32),
+            pltpu.VMEM((16, NBAND), jnp.int32),
+            pltpu.VMEM((4, 2, 8, 512), f32),
+            pltpu.VMEM((2, 64, 512), f32),
+            pltpu.VMEM((4, 2, 512), f32),
+            pltpu.VMEM((2, 128, 128), f32),
+            pltpu.VMEM((2, 64, 64), bf16),
             pltpu.VMEM((2, 512, 256), bf16),
             pltpu.VMEM((2, 256, 1024), bf16),
             pltpu.VMEM((2, 512, 256), bf16),
             pltpu.VMEM((2, 256, 256), bf16),
             pltpu.VMEM((2, 256, 256), bf16),
             pltpu.VMEM((16, 32, 256), bf16),
-            pltpu.VMEM((32 + NQ, 2, 4), jnp.int32),
-            pltpu.SMEM((32 + NQ, 2, 4), jnp.int32),
+            pltpu.VMEM((32, 2, 4), jnp.int32),
+            pltpu.SMEM((32, 2, 4), jnp.int32),
+            pltpu.VMEM((2 * NQ, 2, 4), jnp.int32),
+            pltpu.SMEM((2 * NQ, 2, 4), jnp.int32),
             pltpu.VMEM((32, REACH, 8, 128), bf16),
             pltpu.VMEM((32 * REACH, 8, 128), bf16),
             pltpu.VMEM((2, 256, 128), bf16),
@@ -493,15 +527,15 @@
             pltpu.VMEM((NQ, 4, 4, 128), f32),
             pltpu.VMEM((32, 4, 4, 128), f32),
             pltpu.VMEM((4, 48, 64), f32),
-            sems(5),
-            sems(5),
-            sems(10),
-            sems(18),
+            sems(6),
+            sems(13),
+            sems(11),
+            sems(19),
         ),
         collective=0,
         name="main",
     )(
-        tops, shifts, classes, live, micrograph, consts["row_twist"], consts["box_twist"], consts["box_quarter"], consts["col_twist"],
+        micrograph, shifts, tops, classes, live, consts["row_twist"], consts["box_twist"], consts["box_quarter"], consts["col_twist"],
         consts["box_two"], consts["row_one"], consts["row_two"], consts["box_one"], consts["col_one"], consts["col_two"],
     )
 

time: 72.5 us -> 70.4 us (0.971)
  Pallas kernels: 70.4 us -> 68.4 us
    pallas_call x1, Pallas kernels: 70.4 us -> 68.4 us  [per_device(): call(main_kernel, (pltpu.VMEM((1, 8, NPIX), f32), pltpu.VMEM((CLASSES, 2,...]
where the time goes in v6:
time: 70.4 us; the launch traced here: 70.3 us
  Pallas kernels  68.4 us (97%)
  local copies, waits for them, and re-layouts  1.3 us (2%)
    pallas_call x1, Pallas kernels, per_device(): call(main_kernel, (pltpu.VMEM((1, 8, NPIX), f32), pltpu.VMEM((CLASSES, 2,...  68.4 us

profile of v6, /device:TPU:1, one launch (start us, length us, event | category | flops | bytes accessed | tf_op | source)
XLA Modules:
  0.0 70.3 jit_solution(7426309777827606399)
XLA Ops:
  0.6 68.4 %main.1 = (f32[1,8,4096]{2,1,0:T(8,128)S(1)}, f32[50,2,2,64]{3,2,1,0:T(2,128)S(1)}) custom-call(bf16[32,1024]{1,0:T(8,128)(2,1)} %mic_ref.1, s32[2,4]{1,0:T(2,128)} %bitcast.15, s32[32,128]{1,0:T(8,128)} %bitcast.12, s32[16,128]{1,0:T(8,128)} %bitcast.13, s32[16,128]{1,0:T(8,128)} %bitcast.14, f32[4,2,8,512]{3,2,1,0:T(8,128)} %constant.21.clone.row_twist_hbm, ...), custom_call_target="tpu_custom_call" | custom-call | tf_op jit(solution)/shard_map/main/pallas_call | solution.py:494
  69.0 0.7 copy.19
  69.7 0.6 copy.20

commit v7 on v6

--- a/solution.py
+++ b/solution.py
@@ -350,18 +350,19 @@
     chosen = chosen.T[:64].astype(bf16)
     columns = [mm(chosen, held[:, c, :].astype(bf16)) for c in range(8)]
     main = full_product(box_one_ref, jnp.concatenate([column[:48] for column in columns], axis=0), mmt)
-    rest = full_product(box_one_ref, jnp.concatenate([column[48:50] for column in columns], axis=0), mmt)
-    rest = jnp.concatenate([rest[64 * k : 64 * k + 64] for k in range(NQ)], axis=1)
-    for k in range(NQ):
-        for t in range(3):
+    for t in range(2):
+        for k in range(NQ):
             to_z[NQ * t + k] = main[64 * k : 64 * k + 64, 128 * t : 128 * t + 128].reshape(NZ, 4, 128).astype(bf16)
-    to_z[24] = rest.reshape(NZ, 4, 128).astype(bf16)
-
     for k in far_first(NZ):
         other = lax.rem(z + k, NZ)
         remote(
             to_z.at[pl.ds(0, 16), other], landed.at[pl.ds(0, 16), z], send.at[0], recv.at[0], other * NQ + q, y
         ).start()
+    for k in range(NQ):
+        to_z[2 * NQ + k] = main[64 * k : 64 * k + 64, 256:384].reshape(NZ, 4, 128).astype(bf16)
+    rest = full_product(box_one_ref, jnp.concatenate([column[48:50] for column in columns], axis=0), mmt)
+    rest = jnp.concatenate([rest[64 * k : 64 * k + 64] for k in range(NQ)], axis=1)
+    to_z[24] = rest.reshape(NZ, 4, 128).astype(bf16)
     for k in far_first(NZ):
         other = lax.rem(z + k, NZ)
         remote(

time: 70.4 us -> 70.2 us (level)
  no operation moved by 1% of the time
where the time goes in v7:
time: 70.2 us; the launch traced here: 70.1 us
  Pallas kernels  68.2 us (97%)
  local copies, waits for them, and re-layouts  1.3 us (2%)
    pallas_call x1, Pallas kernels, per_device(): call(main_kernel, (pltpu.VMEM((1, 8, NPIX), f32), pltpu.VMEM((CLASSES, 2,...  68.2 us

profile of v7, /device:TPU:1, one launch (start us, length us, event | category | flops | bytes accessed | tf_op | source)
XLA Modules:
  0.0 70.1 jit_solution(13405293200674315394)
XLA Ops:
  0.6 68.2 %main.1 = (f32[1,8,4096]{2,1,0:T(8,128)S(1)}, f32[50,2,2,64]{3,2,1,0:T(2,128)S(1)}) custom-call(bf16[32,1024]{1,0:T(8,128)(2,1)} %mic_ref.1, s32[2,4]{1,0:T(2,128)} %bitcast.15, s32[32,128]{1,0:T(8,128)} %bitcast.12, s32[16,128]{1,0:T(8,128)} %bitcast.13, s32[16,128]{1,0:T(8,128)} %bitcast.14, f32[4,2,8,512]{3,2,1,0:T(8,128)} %constant.21.clone.row_twist_hbm, ...), custom_call_target="tpu_custom_call" | custom-call | tf_op jit(solution)/shard_map/main/pallas_call | solution.py:495
  68.8 0.7 copy.19
  69.5 0.6 copy.20

commit v8 on v7

--- a/solution.py
+++ b/solution.py
@@ -227,7 +227,7 @@
             strips.append(pltpu.roll(picked, shift, 1))
         boxes[:, d] = jnp.concatenate(strips, axis=0).T.reshape(32, 8, 128).astype(bf16)
 
-    loop(REACH, one_band, unroll=3)
+    loop(REACH, one_band, unroll=9)
 
     here = p * REACH
     for level in range(NQ):
@@ -339,7 +339,7 @@
             wait_for(boxes_in.at[pl.ds(0, 36)], recv.at[8 + g])
         wait_for(boxes_in.at[pl.ds(0, 36)], recv.at[12 + g])
         j = lax.rem(y + g, NY)
-        loop(NQ, lambda q0: one_home(q0, j), unroll=4)
+        loop(NQ, lambda q0: one_home(q0, j), unroll=2)
 
     for load in loads[4:7]:
         load.wait()

time: 70.2 us -> 70.1 us (level)
  no operation moved by 1% of the time
where the time goes in v8:
time: 70.1 us; the launch traced here: 70 us
  Pallas kernels  68.1 us (97%)
  local copies, waits for them, and re-layouts  1.3 us (2%)
    pallas_call x1, Pallas kernels, per_device(): call(main_kernel, (pltpu.VMEM((1, 8, NPIX), f32), pltpu.VMEM((CLASSES, 2,...  68.1 us

profile of v8, /device:TPU:1, one launch (start us, length us, event | category | flops | bytes accessed | tf_op | source)
XLA Modules:
  0.0 70.0 jit_solution(15415672618963940623)
XLA Ops:
  0.6 68.1 %main.1 = (f32[1,8,4096]{2,1,0:T(8,128)S(1)}, f32[50,2,2,64]{3,2,1,0:T(2,128)S(1)}) custom-call(bf16[32,1024]{1,0:T(8,128)(2,1)} %mic_ref.1, s32[2,4]{1,0:T(2,128)} %bitcast.15, s32[32,128]{1,0:T(8,128)} %bitcast.12, s32[16,128]{1,0:T(8,128)} %bitcast.13, s32[16,128]{1,0:T(8,128)} %bitcast.14, f32[4,2,8,512]{3,2,1,0:T(8,128)} %constant.21.clone.row_twist_hbm, ...), custom_call_target="tpu_custom_call" | custom-call | tf_op jit(solution)/shard_map/main/pallas_call | solution.py:495
  68.7 0.7 copy.19
  69.4 0.6 copy.20
